TPU v7x, 256 devices: a whole 4x4x8 slice. The times are simulated.
256 devices in a mesh: dp: 2 (over core), tvoc: 16 (over x, y), svoc: 8 (over z).
Axes of the slice: x: 4, y: 4, z: 8, core: 2. Of those that a mesh axis runs over, the one named last changes fastest.
Arguments:
- teacher_probs: bfloat16 [256, 81920], P('dp', 'tvoc'), may hold values from 0 to 1, as said below
- block_values: bfloat16 [16, 8, 24, 128, 128], P('tvoc', 'svoc'), may hold values from 0.0099487305 to 1
- block_index: int32 [16, 8, 24, 2], P('tvoc', 'svoc'), may hold values from 0 to 63, as said below
- block_count: int32 [16, 8], P('tvoc', 'svoc'), may hold values from 17 to 24, as said below
- hidden: bfloat16 [256, 3072], P('dp'), may hold values from -48 to 48
- student_weight: bfloat16 [3072, 65536], P(None, ('tvoc', 'svoc')), may hold values from -0.15 to 0.15
Outputs:
- divergence: float32 [256], P('dp')
- grad_weight: bfloat16 [3072, 65536], P('dp', ('tvoc', 'svoc'))
- grad_hidden: float32 [256, 3072], P('dp', ('tvoc', 'svoc'))
Inputs may be any that keep to these rules, and one draw needn't show every extreme that they name: `teacher_probs`: each row sums to one and every entry is positive. `block_index`: The live slots of one device name at most 2 distinct c with the same c // 4, and some value of c // 4 reaches 2 on every device. Several live slots may name the same c, with the same or another teacher block. `block_count`: the live slots are the first ones; some device has all 24 live.
All inputs are finite; a program needn't handle non-finite values.
Results may differ from a plain program's by a relative error of at most 0.013.
Values may be sent and summed in bfloat16 or wider, within the bound.
No kernel may reach another device: no remote copies, remote signals or barrier semaphores. Data moves between devices by JAX's collectives and lax.ppermute only.
A program may use at most 64 MiB of HBM per device.

v0:
```python
import jax
import jax.numpy as jnp
from jax import lax
from jax.sharding import Mesh
from jax.sharding import PartitionSpec as P

CAP = 2
TVOC = ("tvoc_0", "tvoc_1")
TVOC_SVOC = ("tvoc_0", "tvoc_1", "svoc")


loss_scale = 128.0


def all_in_one(array, axis):
    leaves = jax.tree.leaves(array)
    sequence = sorted(range(len(leaves)), key=lambda k: -leaves[k].size)
    width = (1, *leaves[sequence[0]].shape)[-1]
    lines = [
        jnp.pad(leaves[k].reshape(-1), (0, -leaves[k].size % width)).reshape(-1, width)
        for k in sequence
    ]
    both, at, found = (lax.all_gather(jnp.concatenate(lines), axis), 0, {})
    for k, line in zip(sequence, lines):
        piece = both[:, at : at + len(line)].reshape(len(both), -1)
        found[k] = piece[:, : leaves[k].size].reshape(-1, *leaves[k].shape)
        at += len(line)
    numbers = iter(range(len(leaves)))
    return jax.tree.map(lambda _: found[next(numbers)], array)


def combined_by_axis(array, axes, combine):
    for axis in axes:
        pieces = all_in_one(array, axis)
        array = jax.tree.map(lambda part: part[0], pieces)
        for k in range(1, lax.axis_size(axis)):
            array = combine(array, jax.tree.map(lambda part: part[k], pieces))
    return array


def split_up(array, dim, length):
    before, after = (array.shape[:dim], array.shape[dim + 1 :])
    return jnp.moveaxis(array.reshape(*before, length, -1, *after), dim, 0)


def sent_and_summed(array, axis, dim):
    parts = split_up(array, dim, lax.axis_size(axis))
    arrived = lax.all_to_all(parts, axis, split_axis=0, concat_axis=0, tiled=True)
    return arrived.astype(jnp.float32).sum(axis=0)


def sum_at_owner(array, axis, dim):
    length = lax.axis_size(axis)
    parts = lax.all_to_all(split_up(array, dim, length), axis, 0, 0, tiled=True)
    return jnp.sum(parts, axis=0)


def sum_in_two_steps(array, axes, dim):
    far, near = axes
    parts = split_up(array, dim, lax.axis_size(far))
    nearer = sum_at_owner(parts, near, dim + 1)
    arrived = lax.all_to_all(nearer, far, split_axis=0, concat_axis=0, tiled=True)
    return arrived.sum(axis=0)


def merge_rows(first, second):
    largest = jnp.maximum(first[0], second[0])
    joined = first[1] * jnp.exp(first[0] - largest) + second[1] * jnp.exp(second[0] - largest)
    return (largest, joined, first[2] + second[2], first[3] + second[3], first[4] + second[4])


def local(teacher_probs, block_values, block_index, block_count, hidden, student_weight):
    tokens = hidden.shape[0]
    block_size = block_values.shape[-1]
    slot_count = block_values.shape[2]
    owners = lax.axis_size(TVOC)
    shard_width = student_weight.shape[1]
    per_owner = shard_width // block_size
    teacher_rows = block_index[0, 0, :, 0]
    block_columns = block_index[0, 0, :, 1]
    occupied = jnp.arange(slot_count, dtype=jnp.int32) < block_count[0, 0]
    teacher_blocks = teacher_probs.reshape(tokens, -1, block_size)
    picked = jnp.take(teacher_blocks, teacher_rows, axis=1)
    mapped = jnp.einsum(
        "tsk,skc->stc", picked, block_values[0, 0], preferred_element_type=jnp.float32
    )
    select = (
        (block_columns[:, None] == jnp.arange(owners * per_owner, dtype=jnp.int32)[None, :])
        & occupied[:, None]
    ).astype(jnp.float32)
    column_used = jnp.max(select, axis=0).reshape(owners, per_owner)
    column_rank = jnp.cumsum(column_used, axis=1) - column_used
    slot_pick = column_used[:, None, :] * (
        column_rank[:, None, :] == jnp.arange(CAP, dtype=jnp.float32)[None, :, None]
    )
    routing = jnp.einsum("sob,ocb->soc", select.reshape(slot_count, owners, per_owner), slot_pick)
    outgoing = jnp.einsum("soc,stk->tock", routing, mapped).astype(jnp.bfloat16)
    positions = jnp.arange(per_owner, dtype=jnp.float32)
    labels = (
        jnp.sum(slot_pick * positions[None, None, :], axis=2) + jnp.sum(slot_pick, axis=2) - 1.0
    )
    received, received_labels = (
        lax.all_to_all(outgoing, TVOC, split_axis=1, concat_axis=1, tiled=True),
        lax.all_to_all(
            labels[None].astype(jnp.bfloat16), TVOC, split_axis=1, concat_axis=1, tiled=True
        ),
    )
    placing = (
        received_labels[0][:, :, None] == positions.astype(jnp.bfloat16)[None, None, :]
    ).astype(jnp.bfloat16)
    teacher_mass = jnp.einsum(
        "scb,tsck->tbk", placing, received, preferred_element_type=jnp.float32
    ).reshape(tokens, shard_width)
    logits = jnp.dot(hidden, student_weight, preferred_element_type=jnp.float32)
    positive = teacher_mass > 0
    entropy_local = jnp.sum(
        jnp.where(positive, teacher_mass * jnp.log(jnp.where(positive, teacher_mass, 1.0)), 0.0),
        axis=1,
    )
    cross_local = jnp.sum(teacher_mass * logits, axis=1)
    mass_local = jnp.sum(teacher_mass, axis=1)
    local_max = jnp.max(logits, axis=1)
    local_exp = jnp.exp(logits - local_max[:, None])
    largest, total, mass_sum, entropy_sum, cross_sum = combined_by_axis(
        (local_max, jnp.sum(local_exp, axis=1), mass_local, entropy_local, cross_local),
        TVOC_SVOC,
        merge_rows,
    )
    shifted = local_exp * jnp.exp(local_max - largest)[:, None]
    divergence = (
        entropy_sum / mass_sum - jnp.log(mass_sum) - cross_sum / mass_sum + largest + jnp.log(total)
    )
    target = teacher_mass / mass_sum[:, None]
    logit_grad = (loss_scale * (shifted / total[:, None] - target)).astype(jnp.bfloat16)
    grad_weight = sent_and_summed(
        lax.dot_general(
            hidden, logit_grad, (((0,), (0,)), ((), ())), preferred_element_type=jnp.float32
        ).astype(jnp.bfloat16),
        "dp",
        0,
    ).astype(jnp.bfloat16)
    grad_hidden = sum_in_two_steps(
        lax.dot_general(
            student_weight, logit_grad, (((1,), (1,)), ((), ())), preferred_element_type=jnp.float32
        ),
        ("tvoc_0", ("tvoc_1", "svoc")),
        0,
    ).T
    return (divergence, grad_weight, grad_hidden)


def solution(mesh):
    finer = Mesh(
        mesh.devices.reshape(mesh.shape["dp"], 4, 4, mesh.shape["svoc"]),
        ("dp", "tvoc_0", "tvoc_1", "svoc"),
    )
    placed = (
        P("dp", TVOC),
        P(TVOC, "svoc", None, None, None),
        P(TVOC, "svoc", None, None),
        P(TVOC, "svoc"),
        P("dp", None),
        P(None, TVOC_SVOC),
    )
    return jax.shard_map(
        local,
        mesh=finer,
        in_specs=placed,
        out_specs=(P("dp"), P("dp", TVOC_SVOC), P("dp", TVOC_SVOC)),
        check_vma=False,
    )
```

profile of v0, /device:TPU:1, one launch (start us, length us, event | category | flops | bytes accessed | tf_op | source)
XLA Modules:
  0.0 166.5 jit_solution(2732076997773196352)
XLA Ops:
  3.4 7.6 %all-to-all-start.1 = ((bf16[1,16,2]{2,0,1:T(2,128)(2,1)}), bf16[1,16,2]{2,0,1:T(2,128)(2,1)S(1)}, u32[]{:S(2)}, u32[]{:S(2)}) async-start(bf16[1,16,2]{2,0,1:T(2,128)(2,1)} %copy.35), calls=%async_computation.1 | async-start | bytes 16384 | tf_op jit(solution)/shard_map/all_to_all | solution.py:104
  12.6 2.4 %copy.29 = bf16[128,5120]{0,1:T(8,128)(2,1)} copy(bf16[128,5120]{1,0:T(8,128)(2,1)} %param.6) | data formatting | bytes 2621440 | tf_op args[0]
  15.0 2.4 %copy.30 = bf16[128,40,128]{2,0,1:T(8,128)(2,1)} copy(bf16[128,40,128]{0,2,1:T(8,128)(2,1)} %bitcast.397) | data formatting | bytes 2621440 | tf_op jit(solution)/shard_map/reshape | solution.py:82
  17.4 2.9 %gather_fusion = bf16[24,128,128]{2,1,0:T(8,128)(2,1)} fusion(bf16[128,40,128]{2,0,1:T(8,128)(2,1)} %copy.30, s32[1024]{0:T(1024)S(1)} %pad_clamp_fusion), kind=kCustom, calls=%fused_computation | custom fusion | bytes 1572960 | tf_op jit(solution)/shard_map/jit(_take)/gather | solution.py:83
  22.7 1.9 %copy.33 = bf16[128,16,2,128]{3,2,0,1:T(2,128)(2,1)} copy(bf16[128,16,2,128]{3,1,2,0:T(8,128)(2,1)S(1)} %fusion.5) | data formatting | bytes 2097152 | tf_op jit(solution)/shard_map/convert_element_type | solution.py:97
  24.6 6.7 %all-to-all-start = ((bf16[128,16,2,128]{3,2,0,1:T(2,128)(2,1)}), bf16[128,16,2,128]{3,2,0,1:T(2,128)(2,1)}, u32[]{:S(2)}, u32[]{:S(2)}) async-start(bf16[128,16,2,128]{3,2,0,1:T(2,128)(2,1)} %copy.33), calls=%async_computation | async-start | bytes 2097152 | tf_op jit(solution)/shard_map/all_to_all | solution.py:103
  31.4 1.8 %fusion.103 = (f32[128]{0:T(128)S(1)}, f32[128,512]{1,0:T(8,128)S(1)}) fusion(bf16[128,3072]{1,0:T(8,128)(2,1)} %param.10, bf16[3072,512]{1,0:T(8,128)(2,1)S(1)} %copy-done), kind=kOutput, calls=%fused_computation.193 | convolution fusion | flops 402718592 | bytes 4194816 | tf_op jit(solution)/shard_map/dot_general | solution.py:114
  33.3 13.4 %all-to-all-done = bf16[128,16,2,128]{3,2,0,1:T(2,128)(2,1)} async-done(((bf16[128,16,2,128]{3,2,0,1:T(2,128)(2,1)}), bf16[128,16,2,128]{3,2,0,1:T(2,128)(2,1)}, u32[]{:S(2)}, u32[]{:S(2)}) %all-to-all-start) | async-done | bytes 1048608 | tf_op jit(solution)/shard_map/all_to_all | solution.py:103
  46.6 2.8 %bitcast_reduce_fusion = (f32[128]{0:T(128)S(1)}, f32[128,128,4,1]{1,2,3,0:T(4,128)S(1)}) fusion(bf16[16,2]{0,1:T(2,128)(2,1)S(1)} %bitcast.409, bf16[4]{0:T(256)(128)(2,1)S(1)} %iota_convert_fusion, bf16[128,16,2,128]{3,2,0,1:T(2,128)(2,1)} %all-to-all-done), kind=kOutput, calls=%fused_computation.27 | convolution fusion | flops 4260096 | bytes 1311304 | tf_op jit(solution)/shard_map/scb,tsck->tbk/dot_general | solution.py:111
  50.7 9.0 %all-gather.3 = f32[4,5,128]{2,1,0:T(8,128)S(1)} all-gather(f32[1,5,128]{2,1,0:T(8,128)S(1)} %bitcast.404), channel_id=2, replica_groups=mesh['dp'=2,'tvoc_0'=4,'tvoc_1'=4,'svoc'=8] {'tvoc_0'}, dimensions={0}, use_global_device_ids=true | all-gather | bytes 12800 | tf_op jit(solution)/shard_map/all_gather | solution.py:23
  59.8 9.0 %all-gather.4 = f32[4,5,128]{2,1,0:T(8,128)S(1)} all-gather(f32[1,5,128]{2,1,0:T(8,128)S(1)} %bitcast.402), channel_id=3, replica_groups=mesh['dp'=2,'tvoc_0'=4,'tvoc_1'=4,'svoc'=8] {'tvoc_1'}, dimensions={0}, use_global_device_ids=true | all-gather | bytes 12800 | tf_op jit(solution)/shard_map/all_gather | solution.py:23
  68.9 21.7 %all-gather.5 = f32[8,5,128]{2,1,0:T(8,128)S(1)} all-gather(f32[1,5,128]{2,1,0:T(8,128)S(1)} %bitcast.403), channel_id=4, replica_groups=mesh['dp'=2,'tvoc_0'=4,'tvoc_1'=4,'svoc'=8] {'svoc'}, dimensions={0}, use_global_device_ids=true | all-gather | bytes 23040 | tf_op jit(solution)/shard_map/all_gather | solution.py:23
  91.2 3.2 %convolution_bitcast_fusion = f32[3072,128]{0,1:T(8,128)} fusion(bf16[3072,512]{1,0:T(8,128)(2,1)S(1)} %copy-done, f32[16,8,4,128]{3,2,1,0:T(4,128)} %bitcast.399, f32[128,512]{1,0:T(8,128)S(1)} %get-tuple-element.29, f32[128]{0:T(128)S(1)} %get-tuple-element.16, f32[128]{0:T(128)S(1)} %get-tuple-element.17, f32[128]{0:T(128)S(1)} %get-tuple-element.13, ...), kind=kOutput, calls=%fused_computation.2 | convolution fusion | flops 403111936 | bytes 5244928 | tf_op jit(solution)/shard_map/dot_general | solution.py:143
  94.5 3.0 %copy.40 = f32[3072,128]{1,0:T(8,128)} copy(f32[3072,128]{0,1:T(8,128)} %convolution_bitcast_fusion) | data formatting | bytes 3145728 | tf_op jit(solution)/shard_map/dot_general | solution.py:143
  97.5 2.7 %copy.41 = f32[32,4,24,128]{3,2,1,0:T(8,128)} copy(f32[32,4,24,128]{3,2,0,1:T(8,128)} %bitcast.396) | data formatting | bytes 3145728 | tf_op jit(solution)/shard_map/transpose | solution.py:43
  100.2 6.0 %all-to-all-start.3 = ((f32[32,4,24,128]{3,2,1,0:T(8,128)}), f32[32,4,24,128]{3,2,1,0:T(8,128)}, u32[]{:S(2)}, u32[]{:S(2)}) async-start(f32[32,4,24,128]{3,2,1,0:T(8,128)} %copy.41), calls=%async_computation.3 | async-start | bytes 3145728 | tf_op jit(solution)/shard_map/all_to_all | solution.py:54
  106.2 2.4 %convolution_convert_fusion = bf16[512,3072]{1,0:T(8,128)(2,1)S(1)} fusion(bf16[128,3072]{1,0:T(8,128)(2,1)} %param.10, f32[16,8,4,128]{3,2,1,0:T(4,128)} %bitcast.400, f32[128,512]{1,0:T(8,128)S(1)} %get-tuple-element.29, f32[128]{0:T(128)S(1)} %get-tuple-element.16, f32[128]{0:T(128)S(1)} %get-tuple-element.17, f32[128]{0:T(128)S(1)} %get-tuple-element.13, ...), kind=kOutput, calls=%fused_computation.1 | convolution fusion | flops 404684800 | bytes 4458496 | tf_op jit(solution)/shard_map/dot_general | solution.py:136
  108.6 1.9 %copy.71 = bf16[64,2,8,1536]{3,2,0,1:T(8,128)(2,1)} copy(bf16[64,2,8,1536]{3,2,1,0:T(8,128)(2,1)S(1)} %bitcast.395) | data formatting | bytes 6291456 | tf_op jit(solution)/shard_map/reshape | solution.py:43
  110.5 17.9 %all-to-all-done.3 = f32[32,4,24,128]{3,2,1,0:T(8,128)} async-done(((f32[32,4,24,128]{3,2,1,0:T(8,128)}), f32[32,4,24,128]{3,2,1,0:T(8,128)}, u32[]{:S(2)}, u32[]{:S(2)}) %all-to-all-start.3) | async-done | bytes 1572896 | tf_op jit(solution)/shard_map/all_to_all | solution.py:54
  128.4 24.2 %all-to-all-start.2 = ((bf16[2,1536,512]{1,2,0:T(8,128)(2,1)}), bf16[2,1536,512]{1,2,0:T(8,128)(2,1)}, u32[]{:S(2)}, u32[]{:S(2)}) async-start(bf16[2,1536,512]{1,2,0:T(8,128)(2,1)} %bitcast.394), calls=%async_computation.2 | async-start | bytes 6291456 | tf_op jit(solution)/shard_map/all_to_all | solution.py:48
  152.6 2.1 %reduce_sum.91 = f32[4,24,128]{2,1,0:T(8,128)} reduce(f32[32,4,24,128]{3,2,1,0:T(8,128)} %all-to-all-done.3, f32[]{:T(128)} %constant.19.clone.1), dimensions={0}, to_apply=%region_10.11 | reduce | flops 380928 | bytes 1622020 | tf_op jit(solution)/shard_map/reduce_sum | solution.py:55
  156.0 3.3 %all-to-all-start.4 = ((f32[4,24,128]{2,1,0:T(8,128)}), f32[4,24,128]{2,1,0:T(8,128)S(1)}, u32[]{:S(2)}, u32[]{:S(2)}) async-start(f32[4,24,128]{2,1,0:T(8,128)} %reduce_sum.91), calls=%async_computation.4 | async-start | bytes 98304 | tf_op jit(solution)/shard_map/all_to_all | solution.py:62
  159.3 4.1 %reduce_sum.90 = bf16[1536,512]{0,1:T(8,128)(2,1)} reduce(bf16[2,1536,512]{1,2,0:T(8,128)(2,1)} %all-to-all-done.2, bf16[]{:T(256)} %constant.36.clone.1), dimensions={0}, to_apply=%region_9.10 | reduce | flops 786432 | bytes 4718594 | tf_op jit(solution)/shard_map/reduce_sum | solution.py:49
  163.3 2.6 %copy.42 = bf16[1536,512]{1,0:T(8,128)(2,1)} copy(bf16[1536,512]{0,1:T(8,128)(2,1)} %reduce_sum.90) | data formatting | bytes 3145728
  (37 shorter events, 9.8 us)
Async XLA Ops:
  0.6 30.7 %copy-start = (bf16[3072,512]{1,0:T(8,128)(2,1)S(1)}, bf16[3072,512]{1,0:T(8,128)(2,1)}, u32[]{:S(2)}) copy-start(bf16[3072,512]{1,0:T(8,128)(2,1)} %param.11) | copy-start | bytes 9437188
  3.4 21.3 %all-to-all-start.1 = ((bf16[1,16,2]{2,0,1:T(2,128)(2,1)}), bf16[1,16,2]{2,0,1:T(2,128)(2,1)S(1)}, u32[]{:S(2)}, u32[]{:S(2)}) async-start(bf16[1,16,2]{2,0,1:T(2,128)(2,1)} %copy.35), calls=%async_computation.1 | async-start | bytes 16384 | tf_op jit(solution)/shard_map/all_to_all | solution.py:104
  24.6 22.0 %all-to-all-start = ((bf16[128,16,2,128]{3,2,0,1:T(2,128)(2,1)}), bf16[128,16,2,128]{3,2,0,1:T(2,128)(2,1)}, u32[]{:S(2)}, u32[]{:S(2)}) async-start(bf16[128,16,2,128]{3,2,0,1:T(2,128)(2,1)} %copy.33), calls=%async_computation | async-start | bytes 2097152 | tf_op jit(solution)/shard_map/all_to_all | solution.py:103
  49.5 1.0 copy-start.1
  100.2 28.1 %all-to-all-start.3 = ((f32[32,4,24,128]{3,2,1,0:T(8,128)}), f32[32,4,24,128]{3,2,1,0:T(8,128)}, u32[]{:S(2)}, u32[]{:S(2)}) async-start(f32[32,4,24,128]{3,2,1,0:T(8,128)} %copy.41), calls=%async_computation.3 | async-start | bytes 3145728 | tf_op jit(solution)/shard_map/all_to_all | solution.py:54
  128.4 27.6 %all-to-all-start.2 = ((bf16[2,1536,512]{1,2,0:T(8,128)(2,1)}), bf16[2,1536,512]{1,2,0:T(8,128)(2,1)}, u32[]{:S(2)}, u32[]{:S(2)}) async-start(bf16[2,1536,512]{1,2,0:T(8,128)(2,1)} %bitcast.394), calls=%async_computation.2 | async-start | bytes 6291456 | tf_op jit(solution)/shard_map/all_to_all | solution.py:48
  156.0 9.9 %all-to-all-start.4 = ((f32[4,24,128]{2,1,0:T(8,128)}), f32[4,24,128]{2,1,0:T(8,128)S(1)}, u32[]{:S(2)}, u32[]{:S(2)}) async-start(f32[4,24,128]{2,1,0:T(8,128)} %reduce_sum.91), calls=%async_computation.4 | async-start | bytes 98304 | tf_op jit(solution)/shard_map/all_to_all | solution.py:62
where the time goes:
time: 167 us; the launch traced here: 166 us
  starting transfers between devices  47.7 us (29%)
  blocking collectives  39.8 us (24%)
  waiting for transfers between devices  32.5 us (19%)
  local copies, waits for them, and re-layouts  21.6 us (13%)
  matrix products  12.8 us (8%)
  other arithmetic  10.4 us (6%)
    all_gather x3, blocking collectives, all_in_one(): both, at, found = (lax.all_gather(jnp.concatenate(lines), axis), 0, {})  39.8 us
    all_to_all x1, starting transfers between devices, sent_and_summed(): lax.all_to_all(parts, axis, split_axis=0, concat_axis=0, tiled=True)  24.2 us
    all_to_all x1, waiting for transfers between devices, sum_at_owner(): parts = lax.all_to_all(split_up(array, dim, length), axis, 0, 0, tiled=True)  17.9 us
    all_to_all x1, waiting for transfers between devices, local(): lax.all_to_all(outgoing, TVOC, split_axis=1, concat_axis=1, tiled=True)  13.4 us
    all_to_all x1, starting transfers between devices, local(): lax.all_to_all(labels[None].astype(jnp.bfloat16), TVOC, split_axis=1, con...  7.58 us
    all_to_all x1, starting transfers between devices, local(): lax.all_to_all(outgoing, TVOC, split_axis=1, concat_axis=1, tiled=True)  6.71 us
    all_to_all x1, starting transfers between devices, sum_at_owner(): parts = lax.all_to_all(split_up(array, dim, length), axis, 0, 0, tiled=True)  5.97 us
    unnamed x6, local copies, waits for them, and re-layouts  5.02 us
  transfers between devices with their start and end apart: 5, of which 3 were waited for; matrix products, arithmetic and copies ran while one was open for 17% of the time, Pallas kernels for 0%

commit v1 on v0

v1 whole, which is shorter than its diff:
```python
import jax
import jax.numpy as jnp
from jax import lax
from jax.experimental import pallas as pl
from jax.experimental.pallas import tpu as pltpu
from jax.sharding import Mesh
from jax.sharding import PartitionSpec as P

CAP = 2
TVOC = ("tvoc_0", "tvoc_1")
TVOC_SVOC = ("tvoc_0", "tvoc_1", "svoc")
LOSS_SCALE = 128.0
F32 = jnp.float32
BF16 = jnp.bfloat16
EXTRA = 8


def vmem():
    return pl.BlockSpec(memory_space=pltpu.VMEM)


def smem():
    return pl.BlockSpec(memory_space=pltpu.SMEM)


def hbm():
    return pl.BlockSpec(memory_space=pltpu.HBM)


def params(limit=20):
    return pltpu.CompilerParams(vmem_limit_bytes=limit << 20)


def as_row(tile):
    return jnp.sum(tile.T, axis=0, keepdims=True)


def lane_blocks(array, width=128):
    return [array[:, k : k + width] for k in range(0, array.shape[1], width)]


def in_parts(row):
    high = row.astype(BF16)
    rest = row - high.astype(F32)
    middle = rest.astype(BF16)
    low = (rest - middle.astype(F32)).astype(BF16)
    return high.astype(F32), middle.astype(F32), low.astype(F32)


def rows_of(parts, height, width):
    at = lax.broadcasted_iota(jnp.int32, (height, width), 0)
    out = jnp.zeros((height, width), F32)
    for k, part in enumerate(parts):
        out = jnp.where(at == k, part, out)
    return out


def before_kernel(
    slots, owners, per_owner, w_parts,
    index, count, probs_h, values_h, hidden_h, weight_h,
    outgoing, logits, stats,
    probs, values, hidden, weight, mapped, first, second, place, sems,
):
    blk = values.shape[-1]
    depth = weight.shape[0] // w_parts
    copies = [
        pltpu.make_async_copy(probs_h, probs, sems.at[0]),
        pltpu.make_async_copy(values_h, values, sems.at[1]),
        pltpu.make_async_copy(hidden_h, hidden, sems.at[2]),
    ] + [
        pltpu.make_async_copy(
            weight_h.at[pl.ds(k * depth, depth)], weight.at[pl.ds(k * depth, depth)], sems.at[3 + k]
        )
        for k in range(w_parts)
    ]
    for copy in copies:
        copy.start()
    for o in range(owners):
        first[o] = -1
        second[o] = -1
    live_slots = count[0]
    for s in range(slots):
        live = s < live_slots
        column = jnp.where(live, index[s, 1], 0)
        owner = column // per_owner
        had = first[owner]
        other = jnp.logical_and(had >= 0, had != column)
        first[owner] = jnp.where(jnp.logical_and(live, had < 0), column, had)
        second[owner] = jnp.where(jnp.logical_and(live, other), column, second[owner])
        place[s] = jnp.where(live, owner * CAP + jnp.where(other, 1, 0), owners * CAP)
    mapped[...] = jnp.zeros_like(mapped)
    copies[0].wait()
    copies[1].wait()
    for s in range(slots):
        row = jnp.where(s < live_slots, index[s, 0], 0)
        at = pl.multiple_of(row * blk, blk)
        block = jnp.dot(probs[:, pl.ds(at, blk)], values[s], preferred_element_type=F32)
        mapped[place[s]] += block
    mass = jnp.zeros((probs.shape[0], blk), F32)
    for o in range(owners):
        for c in range(CAP):
            piece = mapped[o * CAP + c].astype(BF16)
            outgoing[o, c * blk : (c + 1) * blk, :] = piece
            mass = mass + piece.astype(F32)
        label_a = lax.rem(jnp.maximum(first[o], 0), per_owner).astype(F32)
        label_b = lax.rem(jnp.maximum(second[o], 0), per_owner).astype(F32)
        at = lax.broadcasted_iota(jnp.int32, (EXTRA, blk), 0)
        outgoing[o, CAP * blk :, :] = jnp.where(at == 0, label_a, label_b).astype(BF16)
    copies[2].wait()
    total = jnp.zeros(logits.shape, F32)
    for k in range(w_parts):
        copies[3 + k].wait()
        total = total + jnp.dot(
            hidden[:, k * depth : (k + 1) * depth],
            weight[k * depth : (k + 1) * depth, :],
            preferred_element_type=F32,
        )
    logits[...] = total
    parts = lane_blocks(total)
    top = parts[0]
    for part in parts[1:]:
        top = jnp.maximum(top, part)
    largest = jnp.max(top, axis=1, keepdims=True)
    sums = sum(jnp.exp(part - largest) for part in parts)
    largest_row = jnp.max(top.T, axis=0, keepdims=True)
    lse = largest_row + jnp.log(as_row(sums))
    mass_row = as_row(mass)
    both = jnp.concatenate([lse, mass_row], axis=0)
    stats[...] = jnp.broadcast_to(both[None], stats.shape)


def between_kernel(stats, logits, soft, inverse, finals):
    lses = stats[:, 0, :]
    top = jnp.max(lses, axis=0, keepdims=True)
    lse = top + jnp.log(jnp.sum(jnp.exp(lses - top), axis=0, keepdims=True))
    mass = jnp.sum(stats[:, 1, :], axis=0, keepdims=True)
    tokens = lse.shape[1]
    lse_column = jnp.broadcast_to(lse, (tokens, tokens)).T
    inverse[...] = jnp.broadcast_to(LOSS_SCALE / mass, (tokens, tokens)).T
    for k in range(0, logits.shape[1], 128):
        soft[:, k : k + 128] = LOSS_SCALE * jnp.exp(logits[:, k : k + 128] - lse_column)
    finals[...] = jnp.concatenate([1.0 / mass, lse - jnp.log(mass)], axis=0)


def middle_kernel(per_owner, chunks, received, logits, soft, inverse, weight, grad, outgoing):
    sources = received.shape[0]
    blk = received.shape[2]
    scale = inverse[...]
    spread = jnp.zeros(scale.shape, F32)
    masses = [jnp.zeros(scale.shape, F32) for _ in range(per_owner)]
    for s in range(sources):
        labels = received[s, CAP * blk :, :].astype(F32)
        for c in range(CAP):
            label = labels[c : c + 1, :]
            piece = received[s, c * blk : (c + 1) * blk, :].astype(F32)
            for b in range(per_owner):
                masses[b] = masses[b] + jnp.where(label == float(b), piece, 0.0)
    for b in range(per_owner):
        at = slice(b * blk, (b + 1) * blk)
        mass = masses[b]
        positive = mass > 0
        spread = spread + jnp.where(
            positive, mass * (jnp.log(jnp.where(positive, mass, 1.0)) - logits[:, at]), 0.0
        )
        grad[:, at] = (soft[:, at] - mass * scale).astype(BF16)
    tail = rows_of(in_parts(as_row(spread)), EXTRA, blk).astype(BF16)
    owners, height = outgoing.shape[0], outgoing.shape[1] - EXTRA
    step = owners // chunks
    grads = grad[...]
    for k in range(chunks):
        rows = lax.dot_general(
            weight[k * step * height : (k + 1) * step * height, :], grads,
            (((1,), (1,)), ((), ())), preferred_element_type=F32,
        ).astype(BF16)
        for o in range(step):
            outgoing[k * step + o, :height, :] = rows[o * height : (o + 1) * height]
            outgoing[k * step + o, height:, :] = tail


def head_kernel(mine, other, grad_mine, grad_other, out):
    dims = (((0,), (0,)), ((), ()))
    out[...] = (
        lax.dot_general(mine[...], grad_mine[...], dims, preferred_element_type=F32)
        + lax.dot_general(other[...], grad_other[...], dims, preferred_element_type=F32)
    ).astype(BF16)


def half_sum_kernel(received, outgoing):
    total = received[0].astype(F32)
    for s in range(1, received.shape[0]):
        total = total + received[s].astype(F32)
    owners, height = outgoing.shape[0], outgoing.shape[1] - EXTRA
    spread = jnp.sum(total[owners * height : owners * height + 3], axis=0, keepdims=True)
    tail = rows_of(in_parts(spread), EXTRA, total.shape[1]).astype(BF16)
    for o in range(owners):
        outgoing[o, :height, :] = total[o * height : (o + 1) * height].astype(BF16)
        outgoing[o, height:, :] = tail


def last_sum_kernel(received, finals, divergence, grad_hidden):
    total = received[0].astype(F32)
    for s in range(1, received.shape[0]):
        total = total + received[s].astype(F32)
    height = grad_hidden.shape[0]
    grad_hidden[...] = total[:height]
    spread = jnp.sum(total[height : height + 3], axis=0, keepdims=True)
    divergence[...] = spread * finals[0:1, :] + finals[1:2, :]


def local(teacher_probs, block_values, block_index, block_count, hidden, student_weight):
    tokens, width = hidden.shape
    slots, blk = block_values.shape[2], block_values.shape[-1]
    owners, svocs = lax.axis_size(TVOC), lax.axis_size("svoc")
    everyone = owners * svocs
    shard = student_weight.shape[1]
    per_owner = shard // blk
    shape = jax.ShapeDtypeStruct
    w_parts = 6
    half = width // lax.axis_size("dp")
    me = lax.axis_index("dp")
    swap = [(0, 1), (1, 0)]
    hidden_mine = lax.dynamic_slice_in_dim(hidden, me * half, half, 1)
    hidden_other = lax.ppermute(
        lax.dynamic_slice_in_dim(hidden, (1 - me) * half, half, 1), "dp", swap
    )

    def before(*refs):
        before_kernel(slots, owners, per_owner, w_parts, *refs)

    outgoing, logits, stats = pl.pallas_call(
        before,
        out_shape=(
            shape((owners, CAP * blk + EXTRA, blk), BF16),
            shape((tokens, shard), F32),
            shape((everyone, 2, tokens), F32),
        ),
        in_specs=[smem(), smem(), hbm(), hbm(), hbm(), hbm()],
        out_specs=(vmem(), vmem(), vmem()),
        scratch_shapes=[
            pltpu.VMEM(teacher_probs.shape, BF16),
            pltpu.VMEM(block_values.shape[2:], BF16),
            pltpu.VMEM(hidden.shape, BF16),
            pltpu.VMEM(student_weight.shape, BF16),
            pltpu.VMEM((owners * CAP + 1, tokens, blk), F32),
            pltpu.SMEM((owners,), jnp.int32),
            pltpu.SMEM((owners,), jnp.int32),
            pltpu.SMEM((slots,), jnp.int32),
            pltpu.SemaphoreType.DMA((3 + w_parts,)),
        ],
        compiler_params=params(56),
        name="before",
    )(
        block_index[0, 0], block_count[0], teacher_probs, block_values[0, 0], hidden, student_weight
    )
    all_stats = lax.all_to_all(stats, TVOC_SVOC, 0, 0, tiled=True)
    received = lax.all_to_all(outgoing, TVOC, 0, 0, tiled=True)
    soft, inverse, finals = pl.pallas_call(
        between_kernel,
        out_shape=(
            shape((tokens, shard), F32), shape((tokens, tokens), F32), shape((2, tokens), F32),
        ),
        in_specs=[vmem()] * 2,
        out_specs=(vmem(),) * 3,
        compiler_params=params(),
        name="between",
    )(all_stats, logits)

    height = width // owners

    def middle(*refs):
        middle_kernel(per_owner, 4, *refs)

    grad, partial_hidden = pl.pallas_call(
        middle,
        out_shape=(shape((tokens, shard), BF16), shape((owners, height + EXTRA, tokens), BF16)),
        in_specs=[vmem()] * 5,
        out_specs=(vmem(),) * 2,
        compiler_params=params(),
        name="middle",
    )(received, logits, soft, inverse, student_weight)
    grad_other = lax.ppermute(grad, "dp", swap)
    summed = lax.all_to_all(partial_hidden, TVOC, 0, 0, tiled=True)
    tiles = 4
    grad_weight = pl.pallas_call(
        head_kernel,
        out_shape=shape((half, shard), BF16),
        grid=(tiles,),
        in_specs=[
            pl.BlockSpec((tokens, half // tiles), lambda i: (0, i)),
            pl.BlockSpec((tokens, half // tiles), lambda i: (0, i)),
            pl.BlockSpec((tokens, shard), lambda i: (0, 0)),
            pl.BlockSpec((tokens, shard), lambda i: (0, 0)),
        ],
        out_specs=pl.BlockSpec((half // tiles, shard), lambda i: (i, 0)),
        compiler_params=params(),
        name="head",
    )(hidden_mine, hidden_other, grad, grad_other)
    last = height // svocs
    nearer = pl.pallas_call(
        half_sum_kernel,
        out_shape=shape((svocs, last + EXTRA, tokens), BF16),
        in_specs=[vmem()],
        out_specs=vmem(),
        compiler_params=params(),
        name="half_sum",
    )(summed)
    arrived = lax.all_to_all(nearer, "svoc", 0, 0, tiled=True)
    divergence, grad_hidden = pl.pallas_call(
        last_sum_kernel,
        out_shape=(shape((1, tokens), F32), shape((last, tokens), F32)),
        in_specs=[vmem()] * 2,
        out_specs=(vmem(),) * 2,
        compiler_params=params(),
        name="last_sum",
    )(arrived, finals)
    return (divergence[0], grad_weight, grad_hidden.T)


def solution(mesh):
    finer = Mesh(
        mesh.devices.reshape(mesh.shape["dp"], 4, 4, mesh.shape["svoc"]),
        ("dp", "tvoc_0", "tvoc_1", "svoc"),
    )
    placed = (
        P("dp", TVOC),
        P(TVOC, "svoc", None, None, None),
        P(TVOC, "svoc", None, None),
        P(TVOC, "svoc"),
        P("dp", None),
        P(None, TVOC_SVOC),
    )
    return jax.shard_map(
        local,
        mesh=finer,
        in_specs=placed,
        out_specs=(P("dp"), P("dp", TVOC_SVOC), P("dp", TVOC_SVOC)),
        check_vma=False,
    )
```

time: 167 us -> 92 us (0.55)
  the two profiles are of different devices: /device:TPU:1 before, /device:TPU:8 now
where the time goes in v1:
time: 92 us; the launch traced here: 91.5 us
  waiting for transfers between devices  30.5 us (33%)
  blocking collectives  26.8 us (29%)
  starting transfers between devices  14.8 us (16%)
  Pallas kernels  12.5 us (14%)
  local copies, waits for them, and re-layouts  5.42 us (6%)
  between operations  1.39 us (2%)
    all_to_all x1, blocking collectives, local(): all_stats = lax.all_to_all(stats, TVOC_SVOC, 0, 0, tiled=True)  26.8 us
    all_to_all x1, waiting for transfers between devices, local(): received = lax.all_to_all(outgoing, TVOC, 0, 0, tiled=True)  14 us
    all_to_all x1, waiting for transfers between devices, local(): summed = lax.all_to_all(partial_hidden, TVOC, 0, 0, tiled=True)  11 us
    all_to_all x1, starting transfers between devices, local(): received = lax.all_to_all(outgoing, TVOC, 0, 0, tiled=True)  5.9 us
    all_to_all x1, waiting for transfers between devices, local(): arrived = lax.all_to_all(nearer, 'svoc', 0, 0, tiled=True)  5.48 us
    pallas_call x1, Pallas kernels, local(): pl.pallas_call(before, out_shape=(shape((owners, CAP * blk + EXTRA, blk),...  5.27 us
    all_to_all x1, starting transfers between devices, local(): summed = lax.all_to_all(partial_hidden, TVOC, 0, 0, tiled=True)  5 us
    unnamed x16, local copies, waits for them, and re-layouts  4 us
  transfers between devices with their start and end apart: 5, of which 3 were waited for; matrix products, arithmetic and copies ran while one was open for 0% of the time, Pallas kernels for 4%

profile of v1, /device:TPU:8, one launch (start us, length us, event | category | flops | bytes accessed | tf_op | source)
XLA Modules:
  0.0 91.5 jit_solution(3030572195353478297)
XLA Ops:
  0.6 1.4 %copy.9.refs_0_ = s32[24,2]{1,0:T(8,128)} copy(s32[24,2]{0,1:T(2,128)} %bitcast.7) | data formatting | bytes 384 | tf_op jit(solution)/shard_map/squeeze | solution.py:253
  2.6 0.0 copy-start
  2.6 5.3 %before.1 = (bf16[16,264,128]{2,1,0:T(8,128)(2,1)}, f32[128,512]{1,0:T(8,128)}, f32[128,2,128]{2,1,0:T(2,128)}) custom-call(s32[24,2]{1,0:T(8,128)} %copy.9.refs_0_, s32[1]{0:T(128)} %bitcast.5.refs_1_, bf16[128,5120]{1,0:T(8,128)(2,1)} %refs_2_.1, bf16[24,128,128]{2,1,0:T(8,128)(2,1)} %bitcast.6, bf16[128,3072]{1,0:T(8,128)(2,1)} %refs_4_.2, ...), custom_call_target="tpu_custom_call" | custom-call | tf_op jit(solution)/shard_map/before/pallas_call | solution.py:230
  7.9 26.8 %all_to_all.20.stats = f32[128,2,128]{2,1,0:T(2,128)S(1)} all-to-all(f32[128,2,128]{2,1,0:T(2,128)} %get-tuple-element.15), channel_id=1, replica_groups=mesh['dp'=2,'tvoc_0'=4,'tvoc_1'=4,'svoc'=8] {'tvoc_0','tvoc_1','svoc'}, dimensions={0} | all-to-all | bytes 262144 | tf_op jit(solution)/shard_map/all_to_all | solution.py:255
  34.8 5.9 %all-to-all-start = ((bf16[16,264,128]{2,1,0:T(8,128)(2,1)}), bf16[16,264,128]{2,1,0:T(8,128)(2,1)}, u32[]{:S(2)}, u32[]{:S(2)}) async-start(bf16[16,264,128]{2,1,0:T(8,128)(2,1)} %get-tuple-element.13), calls=%async_computation | async-start | bytes 2162688 | tf_op jit(solution)/shard_map/all_to_all | solution.py:256
  40.7 0.2 between.1
  40.9 0.7 copy-done.3
  41.6 0.6 copy-done.5
  42.2 14.0 %all-to-all-done.refs_0_ = bf16[16,264,128]{2,1,0:T(8,128)(2,1)} async-done(((bf16[16,264,128]{2,1,0:T(8,128)(2,1)}), bf16[16,264,128]{2,1,0:T(8,128)(2,1)}, u32[]{:S(2)}, u32[]{:S(2)}) %all-to-all-start) | async-done | bytes 1081376 | tf_op jit(solution)/shard_map/all_to_all | solution.py:256
  56.3 0.9 %copy-done.4 = f32[128,512]{1,0:T(8,128)S(1)} copy-done((f32[128,512]{1,0:T(8,128)S(1)}, f32[128,512]{1,0:T(8,128)}, u32[]{:S(2)}) %copy-start.4) | copy-done | bytes 262168
  57.2 0.8 copy-done.6
  58.1 2.9 %middle.1 = (bf16[128,512]{1,0:T(8,128)(2,1)S(1)}, bf16[16,200,128]{2,1,0:T(8,128)(2,1)S(1)}) custom-call(bf16[16,264,128]{2,1,0:T(8,128)(2,1)} %all-to-all-done.refs_0_, f32[128,512]{1,0:T(8,128)S(1)} %copy-done.1, f32[128,512]{1,0:T(8,128)S(1)} %copy-done.4, f32[128,128]{1,0:T(8,128)S(1)} %copy-done.6, bf16[3072,512]{1,0:T(8,128)(2,1)S(1)} %copy-done), custom_call_target="tpu_custom_call" | custom-call | tf_op jit(solution)/shard_map/middle/pallas_call | solution.py:273
  60.9 0.0 copy-start.2
  61.0 0.9 copy-done.2
  61.8 5.0 %all-to-all-start.2 = ((bf16[16,200,128]{2,1,0:T(8,128)(2,1)}), bf16[16,200,128]{2,1,0:T(8,128)(2,1)S(1)}, u32[]{:S(2)}, u32[]{:S(2)}) async-start(bf16[16,200,128]{2,1,0:T(8,128)(2,1)} %copy-done.2), calls=%async_computation.2 | async-start | bytes 1638400 | tf_op jit(solution)/shard_map/all_to_all | solution.py:282
  66.8 0.1 constant_dynamic-slice_fusion
  66.9 0.1 collective-permute-start
  67.0 0.5 collective-permute-start.1
  67.5 11.0 %all-to-all-done.2.received = bf16[16,200,128]{2,1,0:T(8,128)(2,1)S(1)} async-done(((bf16[16,200,128]{2,1,0:T(8,128)(2,1)}), bf16[16,200,128]{2,1,0:T(8,128)(2,1)S(1)}, u32[]{:S(2)}, u32[]{:S(2)}) %all-to-all-start.2) | async-done | bytes 819232 | tf_op jit(solution)/shard_map/all_to_all | solution.py:282
  78.5 0.7 half_sum.1
  79.2 3.3 %all-to-all-start.3 = ((bf16[8,32,128]{2,1,0:T(8,128)(2,1)}), bf16[8,32,128]{2,1,0:T(8,128)(2,1)S(1)}, u32[]{:S(2)}, u32[]{:S(2)}) async-start(bf16[8,32,128]{2,1,0:T(8,128)(2,1)} %half_sum.1), calls=%async_computation.3 | async-start | bytes 131072 | tf_op jit(solution)/shard_map/all_to_all | solution.py:307
  82.6 2.8 %head.1 = bf16[1536,512]{1,0:T(8,128)(2,1)} custom-call(bf16[128,1536]{1,0:T(8,128)(2,1)S(1)} %get-tuple-element.24.mine, bf16[128,1536]{1,0:T(8,128)(2,1)S(1)} %collective-permute-done.other, bf16[128,512]{1,0:T(8,128)(2,1)S(1)} %get-tuple-element.21.grad_mine, bf16[128,512]{1,0:T(8,128)(2,1)S(1)} %collective-permute-done.1.grad_other), custom_call_target="tpu_custom_call" | custom-call | tf_op jit(solution)/shard_map/head/pallas_call | solution.py:284
  85.4 5.5 %all-to-all-done.3.received = bf16[8,32,128]{2,1,0:T(8,128)(2,1)S(1)} async-done(((bf16[8,32,128]{2,1,0:T(8,128)(2,1)}), bf16[8,32,128]{2,1,0:T(8,128)(2,1)S(1)}, u32[]{:S(2)}, u32[]{:S(2)}) %all-to-all-start.3) | async-done | bytes 65568 | tf_op jit(solution)/shard_map/all_to_all | solution.py:307
  90.9 0.6 last_sum.1
  (11 shorter events, 0.0 us)
Async XLA Ops:
  2.6 53.6 %copy-start = (bf16[3072,512]{1,0:T(8,128)(2,1)S(1)}, bf16[3072,512]{1,0:T(8,128)(2,1)}, u32[]{:S(2)}) copy-start(bf16[3072,512]{1,0:T(8,128)(2,1)} %refs_4_.3) | copy-start | bytes 9437188
  7.9 32.8 %copy-start.1 = (f32[128,512]{1,0:T(8,128)S(1)}, f32[128,512]{1,0:T(8,128)}, u32[]{:S(2)}) copy-start(f32[128,512]{1,0:T(8,128)} %get-tuple-element.14.logits.refs_1_) | copy-start | bytes 786436
  34.8 21.5 %all-to-all-start = ((bf16[16,264,128]{2,1,0:T(8,128)(2,1)}), bf16[16,264,128]{2,1,0:T(8,128)(2,1)}, u32[]{:S(2)}, u32[]{:S(2)}) async-start(bf16[16,264,128]{2,1,0:T(8,128)(2,1)} %get-tuple-element.13), calls=%async_computation | async-start | bytes 2162688 | tf_op jit(solution)/shard_map/all_to_all | solution.py:256
  40.9 0.7 copy-start.3
  41.6 0.6 copy-start.5
  56.3 1.0 %copy-start.4 = (f32[128,512]{1,0:T(8,128)S(1)}, f32[128,512]{1,0:T(8,128)}, u32[]{:S(2)}) copy-start(f32[128,512]{1,0:T(8,128)} %copy-done.3) | copy-start | bytes 786436
  57.2 0.8 copy-start.6
  60.9 0.9 copy-start.2
  61.8 5.0 %copy-start.7 = (bf16[128,3072]{1,0:T(8,128)(2,1)S(1)}, bf16[128,3072]{1,0:T(8,128)(2,1)}, u32[]{:S(2)}) copy-start(bf16[128,3072]{1,0:T(8,128)(2,1)} %refs_4_.2) | copy-start | bytes 2359300
  61.8 16.7 %all-to-all-start.2 = ((bf16[16,200,128]{2,1,0:T(8,128)(2,1)}), bf16[16,200,128]{2,1,0:T(8,128)(2,1)S(1)}, u32[]{:S(2)}, u32[]{:S(2)}) async-start(bf16[16,200,128]{2,1,0:T(8,128)(2,1)} %copy-done.2), calls=%async_computation.2 | async-start | bytes 1638400 | tf_op jit(solution)/shard_map/all_to_all | solution.py:282
  66.9 15.7 %collective-permute-start = (bf16[128,1536]{1,0:T(8,128)(2,1)S(1)}, bf16[128,1536]{1,0:T(8,128)(2,1)S(1)}, u32[]{:S(2)}, u32[]{:S(2)}) collective-permute-start(bf16[128,1536]{1,0:T(8,128)(2,1)S(1)} %get-tuple-element.23), channel_id=1, source_target_pairs={{0,128},{128,0},{1,129},{129,1},{2,130},{130,2},{3,131},{131,3},{4... | collective-permute-start | bytes 1179656 | tf_op jit(solution)/shard_map/ppermute | solution.py:223
  67.0 15.6 %collective-permute-start.1 = (bf16[128,512]{1,0:T(8,128)(2,1)S(1)}, bf16[128,512]{1,0:T(8,128)(2,1)S(1)}, u32[]{:S(2)}, u32[]{:S(2)}) collective-permute-start(bf16[128,512]{1,0:T(8,128)(2,1)S(1)} %get-tuple-element.21.grad_mine), channel_id=1, source_target_pairs={{0,128},{128,0},{1,129},{129,1},{2,130},{130,2},{3,131},{131,3},{4... | collective-permute-start | bytes 393224 | tf_op jit(solution)/shard_map/ppermute | solution.py:281
  79.2 11.7 %all-to-all-start.3 = ((bf16[8,32,128]{2,1,0:T(8,128)(2,1)}), bf16[8,32,128]{2,1,0:T(8,128)(2,1)S(1)}, u32[]{:S(2)}, u32[]{:S(2)}) async-start(bf16[8,32,128]{2,1,0:T(8,128)(2,1)} %half_sum.1), calls=%async_computation.3 | async-start | bytes 131072 | tf_op jit(solution)/shard_map/all_to_all | solution.py:307

commit v2 on v1

--- a/solution.py
+++ b/solution.py
@@ -58,7 +58,7 @@
 def before_kernel(
     slots, owners, per_owner, w_parts,
     index, count, probs_h, values_h, hidden_h, weight_h,
-    outgoing, logits, stats,
+    outgoing, logits, stats, labels,
     probs, values, hidden, weight, mapped, first, second, place, sems,
 ):
     blk = values.shape[-1]
@@ -78,10 +78,10 @@
     for o in range(owners):
         first[o] = -1
         second[o] = -1
-    live_slots = count[0]
+    live_slots = count[0, 0]
     for s in range(slots):
         live = s < live_slots
-        column = jnp.where(live, index[s, 1], 0)
+        column = jnp.where(live, index[1, s], 0)
         owner = column // per_owner
         had = first[owner]
         other = jnp.logical_and(had >= 0, had != column)
@@ -92,7 +92,7 @@
     copies[0].wait()
     copies[1].wait()
     for s in range(slots):
-        row = jnp.where(s < live_slots, index[s, 0], 0)
+        row = jnp.where(s < live_slots, index[0, s], 0)
         at = pl.multiple_of(row * blk, blk)
         block = jnp.dot(probs[:, pl.ds(at, blk)], values[s], preferred_element_type=F32)
         mapped[place[s]] += block
@@ -105,7 +105,7 @@
         label_a = lax.rem(jnp.maximum(first[o], 0), per_owner).astype(F32)
         label_b = lax.rem(jnp.maximum(second[o], 0), per_owner).astype(F32)
         at = lax.broadcasted_iota(jnp.int32, (EXTRA, blk), 0)
-        outgoing[o, CAP * blk :, :] = jnp.where(at == 0, label_a, label_b).astype(BF16)
+        labels[o] = jnp.where(at == 0, label_a, jnp.where(at == 1, label_b, 0.0))
     copies[2].wait()
     total = jnp.zeros(logits.shape, F32)
     for k in range(w_parts):
@@ -129,29 +129,43 @@
     stats[...] = jnp.broadcast_to(both[None], stats.shape)
 
 
-def between_kernel(stats, logits, soft, inverse, finals):
-    lses = stats[:, 0, :]
+def combined(lses, masses):
     top = jnp.max(lses, axis=0, keepdims=True)
     lse = top + jnp.log(jnp.sum(jnp.exp(lses - top), axis=0, keepdims=True))
-    mass = jnp.sum(stats[:, 1, :], axis=0, keepdims=True)
-    tokens = lse.shape[1]
-    lse_column = jnp.broadcast_to(lse, (tokens, tokens)).T
-    inverse[...] = jnp.broadcast_to(LOSS_SCALE / mass, (tokens, tokens)).T
-    for k in range(0, logits.shape[1], 128):
-        soft[:, k : k + 128] = LOSS_SCALE * jnp.exp(logits[:, k : k + 128] - lse_column)
-    finals[...] = jnp.concatenate([1.0 / mass, lse - jnp.log(mass)], axis=0)
-
-
-def middle_kernel(per_owner, chunks, received, logits, soft, inverse, weight, grad, outgoing):
+    return lse, jnp.sum(masses, axis=0, keepdims=True)
+
+
+def tail_kernel(stats, labels, _, outgoing, tails, sem):
+    count = stats.shape[0]
+    lse, mass = combined(
+        jnp.concatenate([stats[k, 0:1, :] for k in range(count)], axis=0),
+        jnp.concatenate([stats[k, 1:2, :] for k in range(count)], axis=0),
+    )
+    blk = lse.shape[1]
+    added = rows_of([0.0, 0.0, *in_parts(lse), *in_parts(mass)], EXTRA, blk)
+    for o in range(tails.shape[0]):
+        tails[o] = (labels[o] + added).astype(BF16)
+    copy = pltpu.make_async_copy(tails, outgoing.at[:, pl.ds(CAP * blk, EXTRA), :], sem)
+    copy.start()
+    copy.wait()
+
+
+def middle_kernel(per_owner, chunks, received, logits, weight, grad, outgoing, finals):
     sources = received.shape[0]
     blk = received.shape[2]
-    scale = inverse[...]
+    tails = [received[s, CAP * blk :, :].astype(F32) for s in range(sources)]
+    lse, mass_sum = combined(
+        jnp.concatenate([jnp.sum(t[2:5], axis=0, keepdims=True) for t in tails], axis=0),
+        jnp.concatenate([jnp.sum(t[5:8], axis=0, keepdims=True) for t in tails], axis=0),
+    )
+    finals[...] = jnp.concatenate([1.0 / mass_sum, lse - jnp.log(mass_sum)], axis=0)
+    lse_column = jnp.broadcast_to(lse, (blk, blk)).T
+    scale = jnp.broadcast_to(LOSS_SCALE / mass_sum, (blk, blk)).T
     spread = jnp.zeros(scale.shape, F32)
     masses = [jnp.zeros(scale.shape, F32) for _ in range(per_owner)]
     for s in range(sources):
-        labels = received[s, CAP * blk :, :].astype(F32)
         for c in range(CAP):
-            label = labels[c : c + 1, :]
+            label = tails[s][c : c + 1, :]
             piece = received[s, c * blk : (c + 1) * blk, :].astype(F32)
             for b in range(per_owner):
                 masses[b] = masses[b] + jnp.where(label == float(b), piece, 0.0)
@@ -162,7 +176,8 @@
         spread = spread + jnp.where(
             positive, mass * (jnp.log(jnp.where(positive, mass, 1.0)) - logits[:, at]), 0.0
         )
-        grad[:, at] = (soft[:, at] - mass * scale).astype(BF16)
+        soft = LOSS_SCALE * jnp.exp(logits[:, at] - lse_column)
+        grad[:, at] = (soft - mass * scale).astype(BF16)
     tail = rows_of(in_parts(as_row(spread)), EXTRA, blk).astype(BF16)
     owners, height = outgoing.shape[0], outgoing.shape[1] - EXTRA
     step = owners // chunks
@@ -211,7 +226,6 @@
     tokens, width = hidden.shape
     slots, blk = block_values.shape[2], block_values.shape[-1]
     owners, svocs = lax.axis_size(TVOC), lax.axis_size("svoc")
-    everyone = owners * svocs
     shard = student_weight.shape[1]
     per_owner = shard // blk
     shape = jax.ShapeDtypeStruct
@@ -227,15 +241,16 @@
     def before(*refs):
         before_kernel(slots, owners, per_owner, w_parts, *refs)
 
-    outgoing, logits, stats = pl.pallas_call(
+    outgoing, logits, stats, labels = pl.pallas_call(
         before,
         out_shape=(
             shape((owners, CAP * blk + EXTRA, blk), BF16),
             shape((tokens, shard), F32),
-            shape((everyone, 2, tokens), F32),
+            shape((svocs, 2, tokens), F32),
+            shape((owners, EXTRA, blk), F32),
         ),
         in_specs=[smem(), smem(), hbm(), hbm(), hbm(), hbm()],
-        out_specs=(vmem(), vmem(), vmem()),
+        out_specs=(vmem(),) * 4,
         scratch_shapes=[
             pltpu.VMEM(teacher_probs.shape, BF16),
             pltpu.VMEM(block_values.shape[2:], BF16),
@@ -250,34 +265,37 @@
         compiler_params=params(56),
         name="before",
     )(
-        block_index[0, 0], block_count[0], teacher_probs, block_values[0, 0], hidden, student_weight
-    )
-    all_stats = lax.all_to_all(stats, TVOC_SVOC, 0, 0, tiled=True)
+        block_index[0, 0].T, block_count, teacher_probs, block_values[0, 0], hidden, student_weight
+    )
+    near_stats = lax.all_to_all(stats, "svoc", 0, 0, tiled=True)
+    outgoing = pl.pallas_call(
+        tail_kernel,
+        out_shape=shape(outgoing.shape, BF16),
+        in_specs=[vmem(), vmem(), hbm()],
+        out_specs=hbm(),
+        scratch_shapes=[pltpu.VMEM((owners, EXTRA, blk), BF16), pltpu.SemaphoreType.DMA],
+        input_output_aliases={2: 0},
+        compiler_params=params(),
+        name="tail",
+    )(near_stats, labels, outgoing)
     received = lax.all_to_all(outgoing, TVOC, 0, 0, tiled=True)
-    soft, inverse, finals = pl.pallas_call(
-        between_kernel,
-        out_shape=(
-            shape((tokens, shard), F32), shape((tokens, tokens), F32), shape((2, tokens), F32),
-        ),
-        in_specs=[vmem()] * 2,
-        out_specs=(vmem(),) * 3,
-        compiler_params=params(),
-        name="between",
-    )(all_stats, logits)
-
     height = width // owners
 
     def middle(*refs):
         middle_kernel(per_owner, 4, *refs)
 
-    grad, partial_hidden = pl.pallas_call(
+    grad, partial_hidden, finals = pl.pallas_call(
         middle,
-        out_shape=(shape((tokens, shard), BF16), shape((owners, height + EXTRA, tokens), BF16)),
-        in_specs=[vmem()] * 5,
-        out_specs=(vmem(),) * 2,
+        out_shape=(
+            shape((tokens, shard), BF16),
+            shape((owners, height + EXTRA, tokens), BF16),
+            shape((2, tokens), F32),
+        ),
+        in_specs=[vmem()] * 3,
+        out_specs=(vmem(),) * 3,
         compiler_params=params(),
         name="middle",
-    )(received, logits, soft, inverse, student_weight)
+    )(received, logits, student_weight)
     grad_other = lax.ppermute(grad, "dp", swap)
     summed = lax.all_to_all(partial_hidden, TVOC, 0, 0, tiled=True)
     tiles = 4

time: 92 us -> 78.8 us (0.86)
  waiting for transfers between devices: 30.5 us -> 15.7 us
  blocking collectives: 26.8 us -> 38.5 us
  starting transfers between devices: 14.8 us -> 8.93 us
  local copies, waits for them, and re-layouts: 5.42 us -> 2.15 us
    all_to_all x1 -> x0, waiting for transfers between devices: 14 us -> none  [local(): received = lax.all_to_all(outgoing, TVOC, 0, 0, tiled=True)]
    all_to_all x1 -> x2, blocking collectives: 26.8 us -> 38.5 us  [the longest x1 22.3 us: local(): received = lax.all_to_all(outgoing, TVOC, 0, 0, tiled=True)]
    all_to_all x1 -> x0, starting transfers between devices: 5.9 us -> none  [local(): received = lax.all_to_all(outgoing, TVOC, 0, 0, tiled=True)]
    unnamed x16 -> x10, local copies, waits for them, and re-layouts: 4 us -> 2.09 us
    squeeze x1 -> x0, local copies, waits for them, and re-layouts: 1.36 us -> none  [local(): block_index[0, 0]]
  transfers between devices with their start and end apart: 5 -> 4, of which waited for: 3 -> 2; matrix products, arithmetic and copies ran while one was open for 0% -> 0% of each run, Pallas kernels for 4% -> 4%
where the time goes in v2:
time: 78.8 us; the launch traced here: 78.4 us
  blocking collectives  38.5 us (49%)
  waiting for transfers between devices  15.7 us (20%)
  Pallas kernels  11.7 us (15%)
  starting transfers between devices  8.93 us (11%)
  local copies, waits for them, and re-layouts  2.15 us (3%)
  between operations  1.35 us (2%)
    all_to_all x1, blocking collectives, local(): received = lax.all_to_all(outgoing, TVOC, 0, 0, tiled=True)  22.3 us
    all_to_all x1, blocking collectives, local(): near_stats = lax.all_to_all(stats, 'svoc', 0, 0, tiled=True)  16.2 us
    all_to_all x1, waiting for transfers between devices, local(): summed = lax.all_to_all(partial_hidden, TVOC, 0, 0, tiled=True)  10.2 us
    all_to_all x1, waiting for transfers between devices, local(): arrived = lax.all_to_all(nearer, 'svoc', 0, 0, tiled=True)  5.5 us
    all_to_all x1, starting transfers between devices, local(): summed = lax.all_to_all(partial_hidden, TVOC, 0, 0, tiled=True)  5 us
    pallas_call x1, Pallas kernels, local(): pl.pallas_call(before, out_shape=(shape((owners, CAP * blk + EXTRA, blk),...  4.64 us
    all_to_all x1, starting transfers between devices, local(): arrived = lax.all_to_all(nearer, 'svoc', 0, 0, tiled=True)  3.35 us
    pallas_call x1, Pallas kernels, local(): pl.pallas_call(middle, out_shape=(shape((tokens, shard), BF16), shape((ow...  2.9 us
  transfers between devices with their start and end apart: 4, of which 2 were waited for; matrix products, arithmetic and copies ran while one was open for 0% of the time, Pallas kernels for 4%

profile of v2, /device:TPU:8, one launch (start us, length us, event | category | flops | bytes accessed | tf_op | source)
XLA Modules:
  0.0 78.4 jit_solution(1770941191710754800)
XLA Ops:
  1.3 4.6 %before.1 = (bf16[16,264,128]{2,1,0:T(8,128)(2,1)}, f32[128,512]{1,0:T(8,128)}, f32[8,2,128]{2,1,0:T(2,128)}, f32[16,8,128]{2,1,0:T(8,128)}) custom-call(s32[2,24]{1,0:T(2,128)} %bitcast.7, s32[1,1]{1,0:T(1,128)S(6)} %copy.11.refs_1_, bf16[128,5120]{1,0:T(8,128)(2,1)} %refs_2_.2, bf16[24,128,128]{2,1,0:T(8,128)(2,1)} %bitcast.6, bf16[128,3072]{1,0:T(8,128)(2,1)} %refs_4_.1, ...), custom_call_target="tpu_custom_call" | custom-call | tf_op jit(solution)/shard_map/before/pallas_call | solution.py:244
  5.9 16.2 %all_to_all.20.stats = f32[8,2,128]{2,1,0:T(2,128)S(1)} all-to-all(f32[8,2,128]{2,1,0:T(2,128)} %get-tuple-element.12), channel_id=1, replica_groups=mesh['dp'=2,'tvoc_0'=4,'tvoc_1'=4,'svoc'=8] {'svoc'}, dimensions={0} | all-to-all | bytes 16384 | tf_op jit(solution)/shard_map/all_to_all | solution.py:270
  22.1 0.0 copy-start.1
  22.1 1.2 %copy-done.1 = bf16[16,264,128]{2,1,0:T(8,128)(2,1)S(1)} copy-done((bf16[16,264,128]{2,1,0:T(8,128)(2,1)S(1)}, bf16[16,264,128]{2,1,0:T(8,128)(2,1)}, u32[]{:S(2)}) %copy-start.1) | copy-done | bytes 1081368
  23.4 0.8 %copy-done.3 = f32[16,8,128]{2,1,0:T(8,128)S(1)} copy-done((f32[16,8,128]{2,1,0:T(8,128)S(1)}, f32[16,8,128]{2,1,0:T(8,128)}, u32[]{:S(2)}) %copy-start.3) | copy-done | bytes 65560
  24.2 0.1 tail.1
  24.3 0.0 copy-start.2
  24.3 22.3 %all_to_all.21.refs_0_ = bf16[16,264,128]{2,1,0:T(8,128)(2,1)S(1)} all-to-all(bf16[16,264,128]{2,1,0:T(8,128)(2,1)S(1)} %tail.1), channel_id=1, replica_groups=mesh['dp'=2,'tvoc_0'=4,'tvoc_1'=4,'svoc'=8] {'tvoc_0','tvoc_1'}, dimensions={0} | all-to-all | bytes 2162688 | tf_op jit(solution)/shard_map/all_to_all | solution.py:281
  46.6 0.0 copy-done
  46.6 0.0 copy-done.2
  46.6 2.9 %middle.1 = (bf16[128,512]{1,0:T(8,128)(2,1)S(1)}, bf16[16,200,128]{2,1,0:T(8,128)(2,1)}, f32[2,128]{1,0:T(2,128)S(1)}) custom-call(bf16[16,264,128]{2,1,0:T(8,128)(2,1)S(1)} %all_to_all.21.refs_0_, f32[128,512]{1,0:T(8,128)S(1)} %copy-done.2, bf16[3072,512]{1,0:T(8,128)(2,1)S(1)} %copy-done), custom_call_target="tpu_custom_call" | custom-call | tf_op jit(solution)/shard_map/middle/pallas_call | solution.py:287
  49.5 5.0 %all-to-all-start.2 = ((bf16[16,200,128]{2,1,0:T(8,128)(2,1)}), bf16[16,200,128]{2,1,0:T(8,128)(2,1)S(1)}, u32[]{:S(2)}, u32[]{:S(2)}) async-start(bf16[16,200,128]{2,1,0:T(8,128)(2,1)} %get-tuple-element.16), calls=%async_computation.2 | async-start | bytes 1638400 | tf_op jit(solution)/shard_map/all_to_all | solution.py:300
  54.5 0.0 copy-done.4
  54.5 0.1 constant_dynamic-slice_fusion
  54.6 0.1 collective-permute-start
  54.7 0.5 collective-permute-start.1
  55.2 10.2 %all-to-all-done.2.received = bf16[16,200,128]{2,1,0:T(8,128)(2,1)S(1)} async-done(((bf16[16,200,128]{2,1,0:T(8,128)(2,1)}), bf16[16,200,128]{2,1,0:T(8,128)(2,1)S(1)}, u32[]{:S(2)}, u32[]{:S(2)}) %all-to-all-start.2) | async-done | bytes 819232 | tf_op jit(solution)/shard_map/all_to_all | solution.py:300
  65.4 0.7 half_sum.1
  66.1 3.3 %all-to-all-start.3 = ((bf16[8,32,128]{2,1,0:T(8,128)(2,1)}), bf16[8,32,128]{2,1,0:T(8,128)(2,1)S(1)}, u32[]{:S(2)}, u32[]{:S(2)}) async-start(bf16[8,32,128]{2,1,0:T(8,128)(2,1)} %half_sum.1), calls=%async_computation.3 | async-start | bytes 131072 | tf_op jit(solution)/shard_map/all_to_all | solution.py:325
  69.5 0.0 collective-permute-done.other
  69.5 0.0 collective-permute-done.1.grad_other
  69.5 2.8 %head.1 = bf16[1536,512]{1,0:T(8,128)(2,1)} custom-call(bf16[128,1536]{1,0:T(8,128)(2,1)S(1)} %get-tuple-element.22.mine, bf16[128,1536]{1,0:T(8,128)(2,1)S(1)} %collective-permute-done.other, bf16[128,512]{1,0:T(8,128)(2,1)S(1)} %get-tuple-element.19.grad_mine, bf16[128,512]{1,0:T(8,128)(2,1)S(1)} %collective-permute-done.1.grad_other), custom_call_target="tpu_custom_call" | custom-call | tf_op jit(solution)/shard_map/head/pallas_call | solution.py:302
  72.3 5.5 %all-to-all-done.3.received = bf16[8,32,128]{2,1,0:T(8,128)(2,1)S(1)} async-done(((bf16[8,32,128]{2,1,0:T(8,128)(2,1)}), bf16[8,32,128]{2,1,0:T(8,128)(2,1)S(1)}, u32[]{:S(2)}, u32[]{:S(2)}) %all-to-all-start.3) | async-done | bytes 65568 | tf_op jit(solution)/shard_map/all_to_all | solution.py:325
  77.8 0.6 last_sum.1
  (3 shorter events, 0.0 us)
Async XLA Ops:
  22.1 1.2 %copy-start.1 = (bf16[16,264,128]{2,1,0:T(8,128)(2,1)S(1)}, bf16[16,264,128]{2,1,0:T(8,128)(2,1)}, u32[]{:S(2)}) copy-start(bf16[16,264,128]{2,1,0:T(8,128)(2,1)} %get-tuple-element.14._) | copy-start | bytes 3244036
  23.4 0.8 %copy-start.3 = (f32[16,8,128]{2,1,0:T(8,128)S(1)}, f32[16,8,128]{2,1,0:T(8,128)}, u32[]{:S(2)}) copy-start(f32[16,8,128]{2,1,0:T(8,128)} %get-tuple-element.13.labels) | copy-start | bytes 196612
  24.2 22.4 %copy-start = (bf16[3072,512]{1,0:T(8,128)(2,1)S(1)}, bf16[3072,512]{1,0:T(8,128)(2,1)}, u32[]{:S(2)}) copy-start(bf16[3072,512]{1,0:T(8,128)(2,1)} %refs_2_.3) | copy-start | bytes 9437188
  24.3 22.3 %copy-start.2 = (f32[128,512]{1,0:T(8,128)S(1)}, f32[128,512]{1,0:T(8,128)}, u32[]{:S(2)}) copy-start(f32[128,512]{1,0:T(8,128)} %get-tuple-element.15.refs_1_) | copy-start | bytes 786436
  49.5 5.0 %copy-start.4 = (bf16[128,3072]{1,0:T(8,128)(2,1)S(1)}, bf16[128,3072]{1,0:T(8,128)(2,1)}, u32[]{:S(2)}) copy-start(bf16[128,3072]{1,0:T(8,128)(2,1)} %refs_4_.1) | copy-start | bytes 2359300
  49.5 15.9 %all-to-all-start.2 = ((bf16[16,200,128]{2,1,0:T(8,128)(2,1)}), bf16[16,200,128]{2,1,0:T(8,128)(2,1)S(1)}, u32[]{:S(2)}, u32[]{:S(2)}) async-start(bf16[16,200,128]{2,1,0:T(8,128)(2,1)} %get-tuple-element.16), calls=%async_computation.2 | async-start | bytes 1638400 | tf_op jit(solution)/shard_map/all_to_all | solution.py:300
  54.6 14.9 %collective-permute-start = (bf16[128,1536]{1,0:T(8,128)(2,1)S(1)}, bf16[128,1536]{1,0:T(8,128)(2,1)S(1)}, u32[]{:S(2)}, u32[]{:S(2)}) collective-permute-start(bf16[128,1536]{1,0:T(8,128)(2,1)S(1)} %get-tuple-element.21), channel_id=1, source_target_pairs={{0,128},{128,0},{1,129},{129,1},{2,130},{130,2},{3,131},{131,3},{4... | collective-permute-start | bytes 1179656 | tf_op jit(solution)/shard_map/ppermute | solution.py:237
  54.7 14.8 %collective-permute-start.1 = (bf16[128,512]{1,0:T(8,128)(2,1)S(1)}, bf16[128,512]{1,0:T(8,128)(2,1)S(1)}, u32[]{:S(2)}, u32[]{:S(2)}) collective-permute-start(bf16[128,512]{1,0:T(8,128)(2,1)S(1)} %get-tuple-element.19.grad_mine), channel_id=1, source_target_pairs={{0,128},{128,0},{1,129},{129,1},{2,130},{130,2},{3,131},{131,3},{4... | collective-permute-start | bytes 393224 | tf_op jit(solution)/shard_map/ppermute | solution.py:299
  66.1 11.7 %all-to-all-start.3 = ((bf16[8,32,128]{2,1,0:T(8,128)(2,1)}), bf16[8,32,128]{2,1,0:T(8,128)(2,1)S(1)}, u32[]{:S(2)}, u32[]{:S(2)}) async-start(bf16[8,32,128]{2,1,0:T(8,128)(2,1)} %half_sum.1), calls=%async_computation.3 | async-start | bytes 131072 | tf_op jit(solution)/shard_map/all_to_all | solution.py:325

commit v3 on v2

--- a/solution.py
+++ b/solution.py
@@ -55,17 +55,17 @@
     return out
 
 
-def before_kernel(
-    slots, owners, per_owner, w_parts,
+def stats_kernel(
+    slots, w_parts,
     index, count, probs_h, values_h, hidden_h, weight_h,
-    outgoing, logits, stats, labels,
-    probs, values, hidden, weight, mapped, first, second, place, sems,
+    logits, stats,
+    probs, values, hidden, weight, sems,
 ):
     blk = values.shape[-1]
     depth = weight.shape[0] // w_parts
     copies = [
-        pltpu.make_async_copy(probs_h, probs, sems.at[0]),
-        pltpu.make_async_copy(values_h, values, sems.at[1]),
+        pltpu.make_async_copy(values_h, values, sems.at[0]),
+        pltpu.make_async_copy(probs_h, probs, sems.at[1]),
         pltpu.make_async_copy(hidden_h, hidden, sems.at[2]),
     ] + [
         pltpu.make_async_copy(
@@ -75,37 +75,16 @@
     ]
     for copy in copies:
         copy.start()
-    for o in range(owners):
-        first[o] = -1
-        second[o] = -1
     live_slots = count[0, 0]
+    copies[0].wait()
+    copies[1].wait()
+    mass = jnp.zeros((probs.shape[0], blk), F32)
     for s in range(slots):
         live = s < live_slots
-        column = jnp.where(live, index[1, s], 0)
-        owner = column // per_owner
-        had = first[owner]
-        other = jnp.logical_and(had >= 0, had != column)
-        first[owner] = jnp.where(jnp.logical_and(live, had < 0), column, had)
-        second[owner] = jnp.where(jnp.logical_and(live, other), column, second[owner])
-        place[s] = jnp.where(live, owner * CAP + jnp.where(other, 1, 0), owners * CAP)
-    mapped[...] = jnp.zeros_like(mapped)
-    copies[0].wait()
-    copies[1].wait()
-    for s in range(slots):
-        row = jnp.where(s < live_slots, index[0, s], 0)
-        at = pl.multiple_of(row * blk, blk)
+        at = pl.multiple_of(jnp.where(live, index[0, s], 0) * blk, blk)
         block = jnp.dot(probs[:, pl.ds(at, blk)], values[s], preferred_element_type=F32)
-        mapped[place[s]] += block
-    mass = jnp.zeros((probs.shape[0], blk), F32)
-    for o in range(owners):
-        for c in range(CAP):
-            piece = mapped[o * CAP + c].astype(BF16)
-            outgoing[o, c * blk : (c + 1) * blk, :] = piece
-            mass = mass + piece.astype(F32)
-        label_a = lax.rem(jnp.maximum(first[o], 0), per_owner).astype(F32)
-        label_b = lax.rem(jnp.maximum(second[o], 0), per_owner).astype(F32)
-        at = lax.broadcasted_iota(jnp.int32, (EXTRA, blk), 0)
-        labels[o] = jnp.where(at == 0, label_a, jnp.where(at == 1, label_b, 0.0))
+        mass = mass + jnp.where(live, block, 0.0)
+    mass_row = as_row(mass)
     copies[2].wait()
     total = jnp.zeros(logits.shape, F32)
     for k in range(w_parts):
@@ -124,9 +103,53 @@
     sums = sum(jnp.exp(part - largest) for part in parts)
     largest_row = jnp.max(top.T, axis=0, keepdims=True)
     lse = largest_row + jnp.log(as_row(sums))
-    mass_row = as_row(mass)
     both = jnp.concatenate([lse, mass_row], axis=0)
     stats[...] = jnp.broadcast_to(both[None], stats.shape)
+
+
+def mapping_kernel(
+    slots, owners, per_owner,
+    index, count, probs_h, values_h,
+    outgoing,
+    probs, values, mapped, first, second, place, sems,
+):
+    blk = values.shape[-1]
+    copies = [
+        pltpu.make_async_copy(values_h, values, sems.at[0]),
+        pltpu.make_async_copy(probs_h, probs, sems.at[1]),
+    ]
+    for copy in copies:
+        copy.start()
+    for o in range(owners):
+        first[o] = -1
+        second[o] = -1
+    live_slots = count[0, 0]
+    for s in range(slots):
+        live = s < live_slots
+        column = jnp.where(live, index[1, s], 0)
+        owner = column // per_owner
+        had = first[owner]
+        other = jnp.logical_and(had >= 0, had != column)
+        first[owner] = jnp.where(jnp.logical_and(live, had < 0), column, had)
+        second[owner] = jnp.where(jnp.logical_and(live, other), column, second[owner])
+        place[s] = jnp.where(live, owner * CAP + jnp.where(other, 1, 0), owners * CAP)
+    mapped[...] = jnp.zeros_like(mapped)
+    for copy in copies:
+        copy.wait()
+    for s in range(slots):
+        row = jnp.where(s < live_slots, index[0, s], 0)
+        at = pl.multiple_of(row * blk, blk)
+        block = jnp.dot(probs[:, pl.ds(at, blk)], values[s], preferred_element_type=F32)
+        mapped[place[s]] += block
+    for o in range(owners):
+        for c in range(CAP):
+            outgoing[o, c * blk : (c + 1) * blk, :] = mapped[o * CAP + c].astype(BF16)
+        label_a = lax.rem(jnp.maximum(first[o], 0), per_owner).astype(F32)
+        label_b = lax.rem(jnp.maximum(second[o], 0), per_owner).astype(F32)
+        at = lax.broadcasted_iota(jnp.int32, (EXTRA, blk), 0)
+        outgoing[o, CAP * blk :, :] = jnp.where(
+            at == 0, label_a, jnp.where(at == 1, label_b, 0.0)
+        ).astype(BF16)
 
 
 def combined(lses, masses):
@@ -135,17 +158,20 @@
     return lse, jnp.sum(masses, axis=0, keepdims=True)
 
 
-def tail_kernel(stats, labels, _, outgoing, tails, sem):
+def tail_kernel(stats, _, outgoing, tails, sems):
+    there = outgoing.at[:, pl.ds(CAP * tails.shape[2], EXTRA), :]
+    labels = pltpu.make_async_copy(there, tails, sems.at[0])
+    labels.start()
     count = stats.shape[0]
     lse, mass = combined(
         jnp.concatenate([stats[k, 0:1, :] for k in range(count)], axis=0),
         jnp.concatenate([stats[k, 1:2, :] for k in range(count)], axis=0),
     )
-    blk = lse.shape[1]
-    added = rows_of([0.0, 0.0, *in_parts(lse), *in_parts(mass)], EXTRA, blk)
+    added = rows_of([0.0, 0.0, *in_parts(lse), *in_parts(mass)], EXTRA, lse.shape[1])
+    labels.wait()
     for o in range(tails.shape[0]):
-        tails[o] = (labels[o] + added).astype(BF16)
-    copy = pltpu.make_async_copy(tails, outgoing.at[:, pl.ds(CAP * blk, EXTRA), :], sem)
+        tails[o] = (tails[o].astype(F32) + added).astype(BF16)
+    copy = pltpu.make_async_copy(tails, there, sems.at[1])
     copy.start()
     copy.wait()
 
@@ -158,7 +184,7 @@
         jnp.concatenate([jnp.sum(t[2:5], axis=0, keepdims=True) for t in tails], axis=0),
         jnp.concatenate([jnp.sum(t[5:8], axis=0, keepdims=True) for t in tails], axis=0),
     )
-    finals[...] = jnp.concatenate([1.0 / mass_sum, lse - jnp.log(mass_sum)], axis=0)
+    finals[...] = lse
     lse_column = jnp.broadcast_to(lse, (blk, blk)).T
     scale = jnp.broadcast_to(LOSS_SCALE / mass_sum, (blk, blk)).T
     spread = jnp.zeros(scale.shape, F32)
@@ -178,7 +204,8 @@
         )
         soft = LOSS_SCALE * jnp.exp(logits[:, at] - lse_column)
         grad[:, at] = (soft - mass * scale).astype(BF16)
-    tail = rows_of(in_parts(as_row(spread)), EXTRA, blk).astype(BF16)
+    sums = [*in_parts(as_row(spread)), *in_parts(as_row(sum(masses[1:], masses[0])))]
+    tail = rows_of(sums, EXTRA, blk).astype(BF16)
     owners, height = outgoing.shape[0], outgoing.shape[1] - EXTRA
     step = owners // chunks
     grads = grad[...]
@@ -205,8 +232,12 @@
     for s in range(1, received.shape[0]):
         total = total + received[s].astype(F32)
     owners, height = outgoing.shape[0], outgoing.shape[1] - EXTRA
-    spread = jnp.sum(total[owners * height : owners * height + 3], axis=0, keepdims=True)
-    tail = rows_of(in_parts(spread), EXTRA, total.shape[1]).astype(BF16)
+    sums = [
+        part
+        for at in (owners * height, owners * height + 3)
+        for part in in_parts(jnp.sum(total[at : at + 3], axis=0, keepdims=True))
+    ]
+    tail = rows_of(sums, EXTRA, total.shape[1]).astype(BF16)
     for o in range(owners):
         outgoing[o, :height, :] = total[o * height : (o + 1) * height].astype(BF16)
         outgoing[o, height:, :] = tail
@@ -219,7 +250,8 @@
     height = grad_hidden.shape[0]
     grad_hidden[...] = total[:height]
     spread = jnp.sum(total[height : height + 3], axis=0, keepdims=True)
-    divergence[...] = spread * finals[0:1, :] + finals[1:2, :]
+    mass = jnp.sum(total[height + 3 : height + 6], axis=0, keepdims=True)
+    divergence[...] = spread / mass - jnp.log(mass) + finals[...]
 
 
 def local(teacher_probs, block_values, block_index, block_count, hidden, student_weight):
@@ -238,46 +270,61 @@
         lax.dynamic_slice_in_dim(hidden, (1 - me) * half, half, 1), "dp", swap
     )
 
-    def before(*refs):
-        before_kernel(slots, owners, per_owner, w_parts, *refs)
-
-    outgoing, logits, stats, labels = pl.pallas_call(
-        before,
-        out_shape=(
-            shape((owners, CAP * blk + EXTRA, blk), BF16),
-            shape((tokens, shard), F32),
-            shape((svocs, 2, tokens), F32),
-            shape((owners, EXTRA, blk), F32),
-        ),
+    index, values = block_index[0, 0].T, block_values[0, 0]
+
+    def stats_of(*refs):
+        stats_kernel(slots, w_parts, *refs)
+
+    logits, stats = pl.pallas_call(
+        stats_of,
+        out_shape=(shape((tokens, shard), F32), shape((svocs, 2, tokens), F32)),
         in_specs=[smem(), smem(), hbm(), hbm(), hbm(), hbm()],
-        out_specs=(vmem(),) * 4,
+        out_specs=(vmem(),) * 2,
         scratch_shapes=[
             pltpu.VMEM(teacher_probs.shape, BF16),
-            pltpu.VMEM(block_values.shape[2:], BF16),
+            pltpu.VMEM(values.shape, BF16),
             pltpu.VMEM(hidden.shape, BF16),
             pltpu.VMEM(student_weight.shape, BF16),
+            pltpu.SemaphoreType.DMA((3 + w_parts,)),
+        ],
+        compiler_params=params(56),
+        name="stats",
+    )(index, block_count, teacher_probs, values, hidden, student_weight)
+    near_stats = lax.all_to_all(stats, "svoc", 0, 0, tiled=True)
+
+    def mapping(*refs):
+        mapping_kernel(slots, owners, per_owner, *refs)
+
+    outgoing = pl.pallas_call(
+        mapping,
+        out_shape=shape((owners, CAP * blk + EXTRA, blk), BF16),
+        in_specs=[smem(), smem(), hbm(), hbm()],
+        out_specs=vmem(),
+        scratch_shapes=[
+            pltpu.VMEM(teacher_probs.shape, BF16),
+            pltpu.VMEM(values.shape, BF16),
             pltpu.VMEM((owners * CAP + 1, tokens, blk), F32),
             pltpu.SMEM((owners,), jnp.int32),
             pltpu.SMEM((owners,), jnp.int32),
             pltpu.SMEM((slots,), jnp.int32),
-            pltpu.SemaphoreType.DMA((3 + w_parts,)),
+            pltpu.SemaphoreType.DMA((2,)),
         ],
-        compiler_params=params(56),
-        name="before",
-    )(
-        block_index[0, 0].T, block_count, teacher_probs, block_values[0, 0], hidden, student_weight
-    )
-    near_stats = lax.all_to_all(stats, "svoc", 0, 0, tiled=True)
+        compiler_params=params(),
+        cost_estimate=pl.CostEstimate(
+            flops=2 * slots * tokens * blk * blk, bytes_accessed=4 << 20, transcendentals=0
+        ),
+        name="mapping",
+    )(index, block_count, teacher_probs, values)
     outgoing = pl.pallas_call(
         tail_kernel,
         out_shape=shape(outgoing.shape, BF16),
-        in_specs=[vmem(), vmem(), hbm()],
+        in_specs=[vmem(), hbm()],
         out_specs=hbm(),
-        scratch_shapes=[pltpu.VMEM((owners, EXTRA, blk), BF16), pltpu.SemaphoreType.DMA],
-        input_output_aliases={2: 0},
+        scratch_shapes=[pltpu.VMEM((owners, EXTRA, blk), BF16), pltpu.SemaphoreType.DMA((2,))],
+        input_output_aliases={1: 0},
         compiler_params=params(),
         name="tail",
-    )(near_stats, labels, outgoing)
+    )(near_stats, outgoing)
     received = lax.all_to_all(outgoing, TVOC, 0, 0, tiled=True)
     height = width // owners
 
@@ -289,7 +336,7 @@
         out_shape=(
             shape((tokens, shard), BF16),
             shape((owners, height + EXTRA, tokens), BF16),
-            shape((2, tokens), F32),
+            shape((1, tokens), F32),
         ),
         in_specs=[vmem()] * 3,
         out_specs=(vmem(),) * 3,

time: 78.8 us -> 76.9 us (0.976)
  blocking collectives: 38.5 us -> 22.3 us
  starting transfers between devices: 8.93 us -> 17.4 us
  waiting for transfers between devices: 15.7 us -> 21.8 us
  local copies, waits for them, and re-layouts: 2.15 us -> 0.08 us
  Pallas kernels: 11.7 us -> 13.5 us
    all_to_all x1 -> x0, blocking collectives: 16.2 us -> none  [local(): near_stats = lax.all_to_all(stats, 'svoc', 0, 0, tiled=True)]
    all_to_all x0 -> x1, starting transfers between devices: none -> 8.48 us  [local(): near_stats = lax.all_to_all(stats, 'svoc', 0, 0, tiled=True)]
    all_to_all x0 -> x1, waiting for transfers between devices: none -> 6.12 us  [local(): near_stats = lax.all_to_all(stats, 'svoc', 0, 0, tiled=True)]
    unnamed x10 -> x12, local copies, waits for them, and re-layouts: 2.09 us -> 0.03 us
    pallas_call x1 -> x2, Pallas kernels: 4.64 us -> 6.34 us  [the longest x1 4.77 us: local(): pl.pallas_call(stats_of, out_shape=(shape((tokens, shard), F32), shape((s...]
  transfers between devices with their start and end apart: 4 -> 5, of which waited for: 2 -> 3; matrix products, arithmetic and copies ran while one was open for 0% -> 0% of each run, Pallas kernels for 4% -> 7%
where the time goes in v3:
time: 76.9 us; the launch traced here: 76.6 us
  blocking collectives  22.3 us (29%)
  waiting for transfers between devices  21.8 us (28%)
  starting transfers between devices  17.4 us (23%)
  Pallas kernels  13.5 us (18%)
  between operations  1.4 us (2%)
    all_to_all x1, blocking collectives, local(): received = lax.all_to_all(outgoing, TVOC, 0, 0, tiled=True)  22.3 us
    all_to_all x1, waiting for transfers between devices, local(): summed = lax.all_to_all(partial_hidden, TVOC, 0, 0, tiled=True)  10.2 us
    all_to_all x1, starting transfers between devices, local(): near_stats = lax.all_to_all(stats, 'svoc', 0, 0, tiled=True)  8.48 us
    all_to_all x1, waiting for transfers between devices, local(): near_stats = lax.all_to_all(stats, 'svoc', 0, 0, tiled=True)  6.12 us
    all_to_all x1, waiting for transfers between devices, local(): arrived = lax.all_to_all(nearer, 'svoc', 0, 0, tiled=True)  5.49 us
    all_to_all x1, starting transfers between devices, local(): summed = lax.all_to_all(partial_hidden, TVOC, 0, 0, tiled=True)  5 us
    pallas_call x1, Pallas kernels, local(): pl.pallas_call(stats_of, out_shape=(shape((tokens, shard), F32), shape((s...  4.77 us
    all_to_all x1, starting transfers between devices, local(): arrived = lax.all_to_all(nearer, 'svoc', 0, 0, tiled=True)  3.35 us
  transfers between devices with their start and end apart: 5, of which 3 were waited for; matrix products, arithmetic and copies ran while one was open for 0% of the time, Pallas kernels for 7%

profile of v3, /device:TPU:8, one launch (start us, length us, event | category | flops | bytes accessed | tf_op | source)
XLA Modules:
  0.0 76.6 jit_solution(2535966840365426793)
XLA Ops:
  1.3 0.0 copy-start.1
  1.3 4.8 %stats.1 = (f32[128,512]{1,0:T(8,128)}, f32[8,2,128]{2,1,0:T(2,128)}) custom-call(s32[2,24]{1,0:T(2,128)} %bitcast.8, s32[1,1]{1,0:T(1,128)S(6)} %copy.11.refs_1_, bf16[128,5120]{1,0:T(8,128)(2,1)} %refs_2_.4, bf16[24,128,128]{2,1,0:T(8,128)(2,1)} %bitcast.6, bf16[128,3072]{1,0:T(8,128)(2,1)} %refs_4_.1, bf16[3072,512]{1,0:T(8,128)(2,1)} %refs_2_.5), custom_call_target="tpu_custom_call" | custom-call | tf_op jit(solution)/shard_map/stats/pallas_call | solution.py:278
  6.1 8.5 %all-to-all-start = ((f32[8,2,128]{2,1,0:T(2,128)}), f32[8,2,128]{2,1,0:T(2,128)S(1)}, u32[]{:S(2)}, u32[]{:S(2)}) async-start(f32[8,2,128]{2,1,0:T(2,128)} %get-tuple-element.10), calls=%async_computation | async-start | bytes 16384 | tf_op jit(solution)/shard_map/all_to_all | solution.py:293
  14.6 0.0 copy-done.2
  14.6 0.0 copy-done.4
  14.6 1.6 %mapping.1._ = bf16[16,264,128]{2,1,0:T(8,128)(2,1)S(1)} custom-call(s32[2,24]{1,0:T(2,128)S(1)} %bitcast.9, s32[1,1]{1,0:T(1,128)S(6)} %copy.11.refs_1_, bf16[128,5120]{1,0:T(8,128)(2,1)S(1)} %copy-done.1, bf16[24,128,128]{2,1,0:T(8,128)(2,1)S(1)} %bitcast.7), custom_call_target="tpu_custom_call" | custom-call | flops 100663296 | bytes 4194304 | tf_op jit(solution)/shard_map/mapping/pallas_call | solution.py:298
  16.2 6.1 %all-to-all-done.stats = f32[8,2,128]{2,1,0:T(2,128)S(1)} async-done(((f32[8,2,128]{2,1,0:T(2,128)}), f32[8,2,128]{2,1,0:T(2,128)S(1)}, u32[]{:S(2)}, u32[]{:S(2)}) %all-to-all-start) | async-done | bytes 8224 | tf_op jit(solution)/shard_map/all_to_all | solution.py:293
  22.3 0.1 tail.1
  22.4 0.0 copy-start.3
  22.4 22.3 %all_to_all.20.refs_0_ = bf16[16,264,128]{2,1,0:T(8,128)(2,1)S(1)} all-to-all(bf16[16,264,128]{2,1,0:T(8,128)(2,1)S(1)} %tail.1), channel_id=1, replica_groups=mesh['dp'=2,'tvoc_0'=4,'tvoc_1'=4,'svoc'=8] {'tvoc_0','tvoc_1'}, dimensions={0} | all-to-all | bytes 2162688 | tf_op jit(solution)/shard_map/all_to_all | solution.py:328
  44.7 0.0 copy-done
  44.7 2.9 %middle.1 = (bf16[128,512]{1,0:T(8,128)(2,1)S(1)}, bf16[16,200,128]{2,1,0:T(8,128)(2,1)}, f32[1,128]{1,0:T(1,128)S(1)}) custom-call(bf16[16,264,128]{2,1,0:T(8,128)(2,1)S(1)} %all_to_all.20.refs_0_, f32[128,512]{1,0:T(8,128)S(1)} %copy-done.3, bf16[3072,512]{1,0:T(8,128)(2,1)S(1)} %copy-done), custom_call_target="tpu_custom_call" | custom-call | tf_op jit(solution)/shard_map/middle/pallas_call | solution.py:334
  47.7 5.0 %all-to-all-start.2 = ((bf16[16,200,128]{2,1,0:T(8,128)(2,1)}), bf16[16,200,128]{2,1,0:T(8,128)(2,1)S(1)}, u32[]{:S(2)}, u32[]{:S(2)}) async-start(bf16[16,200,128]{2,1,0:T(8,128)(2,1)} %get-tuple-element.12), calls=%async_computation.2 | async-start | bytes 1638400 | tf_op jit(solution)/shard_map/all_to_all | solution.py:347
  52.7 0.1 constant_dynamic-slice_fusion
  52.7 0.1 collective-permute-start
  52.8 0.5 collective-permute-start.1
  53.3 10.2 %all-to-all-done.2.received = bf16[16,200,128]{2,1,0:T(8,128)(2,1)S(1)} async-done(((bf16[16,200,128]{2,1,0:T(8,128)(2,1)}), bf16[16,200,128]{2,1,0:T(8,128)(2,1)S(1)}, u32[]{:S(2)}, u32[]{:S(2)}) %all-to-all-start.2) | async-done | bytes 819232 | tf_op jit(solution)/shard_map/all_to_all | solution.py:347
  63.6 0.7 half_sum.1
  64.3 3.3 %all-to-all-start.3 = ((bf16[8,32,128]{2,1,0:T(8,128)(2,1)}), bf16[8,32,128]{2,1,0:T(8,128)(2,1)S(1)}, u32[]{:S(2)}, u32[]{:S(2)}) async-start(bf16[8,32,128]{2,1,0:T(8,128)(2,1)} %half_sum.1), calls=%async_computation.3 | async-start | bytes 131072 | tf_op jit(solution)/shard_map/all_to_all | solution.py:372
  67.7 0.0 collective-permute-done.other
  67.7 0.0 collective-permute-done.1.grad_other
  67.7 2.8 %head.1 = bf16[1536,512]{1,0:T(8,128)(2,1)} custom-call(bf16[128,1536]{1,0:T(8,128)(2,1)S(1)} %get-tuple-element.18.mine, bf16[128,1536]{1,0:T(8,128)(2,1)S(1)} %collective-permute-done.other, bf16[128,512]{1,0:T(8,128)(2,1)S(1)} %get-tuple-element.15.grad_mine, bf16[128,512]{1,0:T(8,128)(2,1)S(1)} %collective-permute-done.1.grad_other), custom_call_target="tpu_custom_call" | custom-call | tf_op jit(solution)/shard_map/head/pallas_call | solution.py:349
  70.5 5.5 %all-to-all-done.3.received = bf16[8,32,128]{2,1,0:T(8,128)(2,1)S(1)} async-done(((bf16[8,32,128]{2,1,0:T(8,128)(2,1)}), bf16[8,32,128]{2,1,0:T(8,128)(2,1)S(1)}, u32[]{:S(2)}, u32[]{:S(2)}) %all-to-all-start.3) | async-done | bytes 65568 | tf_op jit(solution)/shard_map/all_to_all | solution.py:372
  76.0 0.6 last_sum.1
  (7 shorter events, 0.0 us)
Async XLA Ops:
  1.3 13.3 %copy-start.1 = (bf16[128,5120]{1,0:T(8,128)(2,1)S(1)}, bf16[128,5120]{1,0:T(8,128)(2,1)}, u32[]{:S(2)}) copy-start(bf16[128,5120]{1,0:T(8,128)(2,1)} %refs_2_.4) | copy-start | bytes 3932164
  1.3 13.3 %copy-start.2 = (bf16[1,1,24,128,128]{4,3,2,1,0:T(8,128)(2,1)S(1)}, bf16[1,1,24,128,128]{4,3,2,1,0:T(8,128)(2,1)}, u32[]{:S(2)}) copy-start(bf16[1,1,24,128,128]{4,3,2,1,0:T(8,128)(2,1)} %param.7) | copy-start | bytes 2359300
  1.3 13.3 %copy-start.4 = (s32[1,1,24,2]{2,3,1,0:T(2,128)S(1)}, s32[1,1,24,2]{2,3,1,0:T(2,128)}, u32[]{:S(2)}) copy-start(s32[1,1,24,2]{2,3,1,0:T(2,128)} %param.8) | copy-start | bytes 580
  6.1 16.2 %all-to-all-start = ((f32[8,2,128]{2,1,0:T(2,128)}), f32[8,2,128]{2,1,0:T(2,128)S(1)}, u32[]{:S(2)}, u32[]{:S(2)}) async-start(f32[8,2,128]{2,1,0:T(2,128)} %get-tuple-element.10), calls=%async_computation | async-start | bytes 16384 | tf_op jit(solution)/shard_map/all_to_all | solution.py:293
  22.3 22.4 %copy-start = (bf16[3072,512]{1,0:T(8,128)(2,1)S(1)}, bf16[3072,512]{1,0:T(8,128)(2,1)}, u32[]{:S(2)}) copy-start(bf16[3072,512]{1,0:T(8,128)(2,1)} %refs_2_.5) | copy-start | bytes 9437188
  22.4 22.3 %copy-start.3 = (f32[128,512]{1,0:T(8,128)S(1)}, f32[128,512]{1,0:T(8,128)}, u32[]{:S(2)}) copy-start(f32[128,512]{1,0:T(8,128)} %get-tuple-element.11.refs_1_) | copy-start | bytes 786436
  47.7 5.0 %copy-start.5 = (bf16[128,3072]{1,0:T(8,128)(2,1)S(1)}, bf16[128,3072]{1,0:T(8,128)(2,1)}, u32[]{:S(2)}) copy-start(bf16[128,3072]{1,0:T(8,128)(2,1)} %refs_4_.1) | copy-start | bytes 2359300
  47.7 15.9 %all-to-all-start.2 = ((bf16[16,200,128]{2,1,0:T(8,128)(2,1)}), bf16[16,200,128]{2,1,0:T(8,128)(2,1)S(1)}, u32[]{:S(2)}, u32[]{:S(2)}) async-start(bf16[16,200,128]{2,1,0:T(8,128)(2,1)} %get-tuple-element.12), calls=%async_computation.2 | async-start | bytes 1638400 | tf_op jit(solution)/shard_map/all_to_all | solution.py:347
  52.7 14.9 %collective-permute-start = (bf16[128,1536]{1,0:T(8,128)(2,1)S(1)}, bf16[128,1536]{1,0:T(8,128)(2,1)S(1)}, u32[]{:S(2)}, u32[]{:S(2)}) collective-permute-start(bf16[128,1536]{1,0:T(8,128)(2,1)S(1)} %get-tuple-element.17), channel_id=1, source_target_pairs={{0,128},{128,0},{1,129},{129,1},{2,130},{130,2},{3,131},{131,3},{4... | collective-permute-start | bytes 1179656 | tf_op jit(solution)/shard_map/ppermute | solution.py:269
  52.8 14.8 %collective-permute-start.1 = (bf16[128,512]{1,0:T(8,128)(2,1)S(1)}, bf16[128,512]{1,0:T(8,128)(2,1)S(1)}, u32[]{:S(2)}, u32[]{:S(2)}) collective-permute-start(bf16[128,512]{1,0:T(8,128)(2,1)S(1)} %get-tuple-element.15.grad_mine), channel_id=1, source_target_pairs={{0,128},{128,0},{1,129},{129,1},{2,130},{130,2},{3,131},{131,3},{4... | collective-permute-start | bytes 393224 | tf_op jit(solution)/shard_map/ppermute | solution.py:346
  64.3 11.7 %all-to-all-start.3 = ((bf16[8,32,128]{2,1,0:T(8,128)(2,1)}), bf16[8,32,128]{2,1,0:T(8,128)(2,1)S(1)}, u32[]{:S(2)}, u32[]{:S(2)}) async-start(bf16[8,32,128]{2,1,0:T(8,128)(2,1)} %half_sum.1), calls=%async_computation.3 | async-start | bytes 131072 | tf_op jit(solution)/shard_map/all_to_all | solution.py:372

commit v4 on v3

--- a/solution.py
+++ b/solution.py
@@ -19,10 +19,6 @@
     return pl.BlockSpec(memory_space=pltpu.VMEM)
 
 
-def smem():
-    return pl.BlockSpec(memory_space=pltpu.SMEM)
-
-
 def hbm():
     return pl.BlockSpec(memory_space=pltpu.HBM)
 
@@ -57,12 +53,16 @@
 
 def stats_kernel(
     slots, w_parts,
-    index, count, probs_h, values_h, hidden_h, weight_h,
-    logits, stats,
-    probs, values, hidden, weight, sems,
+    index_h, count_h, probs_h, values_h, hidden_h, weight_h,
+    logits_h, stats,
+    index, count, probs, values, hidden, weight, logits, sems,
 ):
     blk = values.shape[-1]
     depth = weight.shape[0] // w_parts
+    small = [
+        pltpu.make_async_copy(index_h, index, sems.at[3 + w_parts]),
+        pltpu.make_async_copy(count_h, count, sems.at[4 + w_parts]),
+    ]
     copies = [
         pltpu.make_async_copy(values_h, values, sems.at[0]),
         pltpu.make_async_copy(probs_h, probs, sems.at[1]),
@@ -73,8 +73,10 @@
         )
         for k in range(w_parts)
     ]
-    for copy in copies:
+    for copy in small + copies:
         copy.start()
+    for copy in small:
+        copy.wait()
     live_slots = count[0, 0]
     copies[0].wait()
     copies[1].wait()
@@ -95,6 +97,8 @@
             preferred_element_type=F32,
         )
     logits[...] = total
+    leaving = pltpu.make_async_copy(logits, logits_h, sems.at[5 + w_parts])
+    leaving.start()
     parts = lane_blocks(total)
     top = parts[0]
     for part in parts[1:]:
@@ -105,24 +109,31 @@
     lse = largest_row + jnp.log(as_row(sums))
     both = jnp.concatenate([lse, mass_row], axis=0)
     stats[...] = jnp.broadcast_to(both[None], stats.shape)
+    leaving.wait()
 
 
 def mapping_kernel(
     slots, owners, per_owner,
-    index, count, probs_h, values_h,
+    index_h, count_h, probs_h, values_h,
     outgoing,
-    probs, values, mapped, first, second, place, sems,
+    index, count, probs, values, mapped, first, second, place, sems,
 ):
     blk = values.shape[-1]
+    small = [
+        pltpu.make_async_copy(index_h, index, sems.at[2]),
+        pltpu.make_async_copy(count_h, count, sems.at[3]),
+    ]
     copies = [
         pltpu.make_async_copy(values_h, values, sems.at[0]),
         pltpu.make_async_copy(probs_h, probs, sems.at[1]),
     ]
-    for copy in copies:
+    for copy in small + copies:
         copy.start()
     for o in range(owners):
         first[o] = -1
         second[o] = -1
+    for copy in small:
+        copy.wait()
     live_slots = count[0, 0]
     for s in range(slots):
         live = s < live_slots
@@ -278,16 +289,19 @@
     logits, stats = pl.pallas_call(
         stats_of,
         out_shape=(shape((tokens, shard), F32), shape((svocs, 2, tokens), F32)),
-        in_specs=[smem(), smem(), hbm(), hbm(), hbm(), hbm()],
-        out_specs=(vmem(),) * 2,
+        in_specs=[hbm()] * 6,
+        out_specs=(hbm(), vmem()),
         scratch_shapes=[
+            pltpu.SMEM(index.shape, jnp.int32),
+            pltpu.SMEM(block_count.shape, jnp.int32),
             pltpu.VMEM(teacher_probs.shape, BF16),
             pltpu.VMEM(values.shape, BF16),
             pltpu.VMEM(hidden.shape, BF16),
             pltpu.VMEM(student_weight.shape, BF16),
-            pltpu.SemaphoreType.DMA((3 + w_parts,)),
+            pltpu.VMEM((tokens, shard), F32),
+            pltpu.SemaphoreType.DMA((6 + w_parts,)),
         ],
-        compiler_params=params(56),
+        compiler_params=params(60),
         name="stats",
     )(index, block_count, teacher_probs, values, hidden, student_weight)
     near_stats = lax.all_to_all(stats, "svoc", 0, 0, tiled=True)
@@ -298,16 +312,18 @@
     outgoing = pl.pallas_call(
         mapping,
         out_shape=shape((owners, CAP * blk + EXTRA, blk), BF16),
-        in_specs=[smem(), smem(), hbm(), hbm()],
+        in_specs=[hbm()] * 4,
         out_specs=vmem(),
         scratch_shapes=[
+            pltpu.SMEM(index.shape, jnp.int32),
+            pltpu.SMEM(block_count.shape, jnp.int32),
             pltpu.VMEM(teacher_probs.shape, BF16),
             pltpu.VMEM(values.shape, BF16),
             pltpu.VMEM((owners * CAP + 1, tokens, blk), F32),
             pltpu.SMEM((owners,), jnp.int32),
             pltpu.SMEM((owners,), jnp.int32),
             pltpu.SMEM((slots,), jnp.int32),
-            pltpu.SemaphoreType.DMA((2,)),
+            pltpu.SemaphoreType.DMA((4,)),
         ],
         compiler_params=params(),
         cost_estimate=pl.CostEstimate(
@@ -361,6 +377,7 @@
         name="head",
     )(hidden_mine, hidden_other, grad, grad_other)
     last = height // svocs
+    summed, grad_weight = lax.optimization_barrier((summed, grad_weight))
     nearer = pl.pallas_call(
         half_sum_kernel,
         out_shape=shape((svocs, last + EXTRA, tokens), BF16),

time: 76.9 us -> 75.2 us (0.978)
  blocking collectives: 22.3 us -> 33.1 us
  waiting for transfers between devices: 21.8 us -> 13.7 us
  starting transfers between devices: 17.4 us -> 14.1 us
  Pallas kernels: 13.5 us -> 12.6 us
    all_to_all x0 -> x1, blocking collectives: none -> 10.8 us  [local(): arrived = lax.all_to_all(nearer, 'svoc', 0, 0, tiled=True)]
    all_to_all x1 -> x0, waiting for transfers between devices: 5.49 us -> none  [local(): arrived = lax.all_to_all(nearer, 'svoc', 0, 0, tiled=True)]
    all_to_all x1, waiting for transfers between devices: 10.2 us -> 6.05 us  [local(): summed = lax.all_to_all(partial_hidden, TVOC, 0, 0, tiled=True)]
    all_to_all x1 -> x0, starting transfers between devices: 3.35 us -> none  [local(): arrived = lax.all_to_all(nearer, 'svoc', 0, 0, tiled=True)]
    ppermute x1, waiting for transfers between devices: 0.01 us -> 1.21 us  [local(): lax.ppermute(lax.dynamic_slice_in_dim(hidden, (1 - me) * half, half, 1),...]
  transfers between devices with their start and end apart: 5 -> 4, of which waited for: 3 -> 4; matrix products, arithmetic and copies ran while one was open for 0% -> 0% of each run, Pallas kernels for 7% -> 6%
where the time goes in v4:
time: 75.2 us; the launch traced here: 74.9 us
  blocking collectives  33.1 us (44%)
  starting transfers between devices  14.1 us (19%)
  waiting for transfers between devices  13.7 us (18%)
  Pallas kernels  12.6 us (17%)
  between operations  1.38 us (2%)
    all_to_all x1, blocking collectives, local(): received = lax.all_to_all(outgoing, TVOC, 0, 0, tiled=True)  22.3 us
    all_to_all x1, blocking collectives, local(): arrived = lax.all_to_all(nearer, 'svoc', 0, 0, tiled=True)  10.8 us
    all_to_all x1, starting transfers between devices, local(): near_stats = lax.all_to_all(stats, 'svoc', 0, 0, tiled=True)  8.49 us
    all_to_all x1, waiting for transfers between devices, local(): near_stats = lax.all_to_all(stats, 'svoc', 0, 0, tiled=True)  6.24 us
    all_to_all x1, waiting for transfers between devices, local(): summed = lax.all_to_all(partial_hidden, TVOC, 0, 0, tiled=True)  6.05 us
    all_to_all x1, starting transfers between devices, local(): summed = lax.all_to_all(partial_hidden, TVOC, 0, 0, tiled=True)  5 us
    pallas_call x1, Pallas kernels, local(): pl.pallas_call(stats_of, out_shape=(shape((tokens, shard), F32), shape((s...  4.59 us
    pallas_call x1, Pallas kernels, local(): pl.pallas_call(middle, out_shape=(shape((tokens, shard), BF16), shape((ow...  2.95 us
  transfers between devices with their start and end apart: 4, of which 4 were waited for; matrix products, arithmetic and copies ran while one was open for 0% of the time, Pallas kernels for 6%

profile of v4, /device:TPU:8, one launch (start us, length us, event | category | flops | bytes accessed | tf_op | source)
XLA Modules:
  0.0 74.9 jit_solution(9520245463316641704)
XLA Ops:
  1.3 0.0 copy-start.1
  1.3 0.0 copy-start.2
  1.3 0.0 copy-start.4
  1.3 4.6 %stats.1 = (f32[128,512]{1,0:T(8,128)}, f32[8,2,128]{2,1,0:T(2,128)}) custom-call(s32[2,24]{1,0:T(2,128)} %bitcast.8, s32[1,1]{1,0:T(1,128)S(6)} %copy.11.refs_1_, bf16[128,5120]{1,0:T(8,128)(2,1)} %refs_2_.4, bf16[24,128,128]{2,1,0:T(8,128)(2,1)} %bitcast.6, bf16[128,3072]{1,0:T(8,128)(2,1)} %refs_4_.1, bf16[3072,512]{1,0:T(8,128)(2,1)} %refs_2_.5), custom_call_target="tpu_custom_call" | custom-call | tf_op jit(solution)/shard_map/stats/pallas_call | solution.py:289
  5.9 8.5 %all-to-all-start = ((f32[8,2,128]{2,1,0:T(2,128)}), f32[8,2,128]{2,1,0:T(2,128)S(1)}, u32[]{:S(2)}, u32[]{:S(2)}) async-start(f32[8,2,128]{2,1,0:T(2,128)} %get-tuple-element.12), calls=%async_computation | async-start | bytes 16384 | tf_op jit(solution)/shard_map/all_to_all | solution.py:307
  14.4 0.0 copy-done.1
  14.4 0.0 copy-done.2
  14.4 1.4 %mapping.1._ = bf16[16,264,128]{2,1,0:T(8,128)(2,1)S(1)} custom-call(s32[2,24]{1,0:T(2,128)S(1)} %bitcast.9, s32[1,1]{1,0:T(1,128)S(6)} %copy.11.refs_1_, bf16[128,5120]{1,0:T(8,128)(2,1)S(1)} %copy-done.1, bf16[24,128,128]{2,1,0:T(8,128)(2,1)S(1)} %bitcast.7), custom_call_target="tpu_custom_call" | custom-call | flops 100663296 | bytes 4194304 | tf_op jit(solution)/shard_map/mapping/pallas_call | solution.py:312
  15.9 6.2 %all-to-all-done.stats = f32[8,2,128]{2,1,0:T(2,128)S(1)} async-done(((f32[8,2,128]{2,1,0:T(2,128)}), f32[8,2,128]{2,1,0:T(2,128)S(1)}, u32[]{:S(2)}, u32[]{:S(2)}) %all-to-all-start) | async-done | bytes 8224 | tf_op jit(solution)/shard_map/all_to_all | solution.py:307
  22.1 0.1 tail.1
  22.2 0.0 copy-start.3
  22.2 22.3 %all_to_all.20.refs_0_ = bf16[16,264,128]{2,1,0:T(8,128)(2,1)S(1)} all-to-all(bf16[16,264,128]{2,1,0:T(8,128)(2,1)S(1)} %tail.1), channel_id=1, replica_groups=mesh['dp'=2,'tvoc_0'=4,'tvoc_1'=4,'svoc'=8] {'tvoc_0','tvoc_1'}, dimensions={0} | all-to-all | bytes 2162688 | tf_op jit(solution)/shard_map/all_to_all | solution.py:344
  44.6 3.0 %middle.1 = (bf16[128,512]{1,0:T(8,128)(2,1)S(1)}, bf16[16,200,128]{2,1,0:T(8,128)(2,1)}, f32[1,128]{1,0:T(1,128)S(1)}) custom-call(bf16[16,264,128]{2,1,0:T(8,128)(2,1)S(1)} %all_to_all.20.refs_0_, f32[128,512]{1,0:T(8,128)S(1)} %copy-done.3, bf16[3072,512]{1,0:T(8,128)(2,1)S(1)} %copy-done), custom_call_target="tpu_custom_call" | custom-call | tf_op jit(solution)/shard_map/middle/pallas_call | solution.py:350
  47.5 5.0 %all-to-all-start.2 = ((bf16[16,200,128]{2,1,0:T(8,128)(2,1)}), bf16[16,200,128]{2,1,0:T(8,128)(2,1)S(1)}, u32[]{:S(2)}, u32[]{:S(2)}) async-start(bf16[16,200,128]{2,1,0:T(8,128)(2,1)} %get-tuple-element.14), calls=%async_computation.2 | async-start | bytes 1638400 | tf_op jit(solution)/shard_map/all_to_all | solution.py:363
  52.5 0.1 constant_dynamic-slice_fusion
  52.6 0.1 collective-permute-start
  52.7 0.5 collective-permute-start.1
  53.2 1.2 %collective-permute-done.other = bf16[128,1536]{1,0:T(8,128)(2,1)S(1)} collective-permute-done((bf16[128,1536]{1,0:T(8,128)(2,1)S(1)}, bf16[128,1536]{1,0:T(8,128)(2,1)S(1)}, u32[]{:S(2)}, u32[]{:S(2)}) %collective-permute-start) | collective-permute-done | bytes 393248 | tf_op jit(solution)/shard_map/ppermute | solution.py:280
  54.4 0.2 collective-permute-done.1.grad_other
  54.6 2.8 %head.1 = bf16[1536,512]{1,0:T(8,128)(2,1)} custom-call(bf16[128,1536]{1,0:T(8,128)(2,1)S(1)} %get-tuple-element.22.mine, bf16[128,1536]{1,0:T(8,128)(2,1)S(1)} %collective-permute-done.other, bf16[128,512]{1,0:T(8,128)(2,1)S(1)} %get-tuple-element.15.grad_mine, bf16[128,512]{1,0:T(8,128)(2,1)S(1)} %collective-permute-done.1.grad_other), custom_call_target="tpu_custom_call" | custom-call | tf_op jit(solution)/shard_map/head/pallas_call | solution.py:365
  57.4 6.1 %all-to-all-done.2.received = bf16[16,200,128]{2,1,0:T(8,128)(2,1)S(1)} async-done(((bf16[16,200,128]{2,1,0:T(8,128)(2,1)}), bf16[16,200,128]{2,1,0:T(8,128)(2,1)S(1)}, u32[]{:S(2)}, u32[]{:S(2)}) %all-to-all-start.2) | async-done | bytes 819232 | tf_op jit(solution)/shard_map/all_to_all | solution.py:363
  63.4 0.1 half_sum.1
  63.5 10.8 %all_to_all.21.received = bf16[8,32,128]{2,1,0:T(8,128)(2,1)S(1)} all-to-all(bf16[8,32,128]{2,1,0:T(8,128)(2,1)S(1)} %half_sum.1), channel_id=1, replica_groups=mesh['dp'=2,'tvoc_0'=4,'tvoc_1'=4,'svoc'=8] {'svoc'}, dimensions={0} | all-to-all | bytes 131072 | tf_op jit(solution)/shard_map/all_to_all | solution.py:389
  74.3 0.6 last_sum.1
  (6 shorter events, 0.0 us)
Async XLA Ops:
  1.3 13.1 %copy-start.1 = (bf16[128,5120]{1,0:T(8,128)(2,1)S(1)}, bf16[128,5120]{1,0:T(8,128)(2,1)}, u32[]{:S(2)}) copy-start(bf16[128,5120]{1,0:T(8,128)(2,1)} %refs_2_.4) | copy-start | bytes 3932164
  1.3 13.1 %copy-start.2 = (bf16[1,1,24,128,128]{4,3,2,1,0:T(8,128)(2,1)S(1)}, bf16[1,1,24,128,128]{4,3,2,1,0:T(8,128)(2,1)}, u32[]{:S(2)}) copy-start(bf16[1,1,24,128,128]{4,3,2,1,0:T(8,128)(2,1)} %param.7) | copy-start | bytes 2359300
  1.3 13.1 %copy-start.4 = (s32[1,1,24,2]{2,3,1,0:T(2,128)S(1)}, s32[1,1,24,2]{2,3,1,0:T(2,128)}, u32[]{:S(2)}) copy-start(s32[1,1,24,2]{2,3,1,0:T(2,128)} %param.8) | copy-start | bytes 580
  5.9 16.2 %all-to-all-start = ((f32[8,2,128]{2,1,0:T(2,128)}), f32[8,2,128]{2,1,0:T(2,128)S(1)}, u32[]{:S(2)}, u32[]{:S(2)}) async-start(f32[8,2,128]{2,1,0:T(2,128)} %get-tuple-element.12), calls=%async_computation | async-start | bytes 16384 | tf_op jit(solution)/shard_map/all_to_all | solution.py:307
  22.1 22.4 %copy-start = (bf16[3072,512]{1,0:T(8,128)(2,1)S(1)}, bf16[3072,512]{1,0:T(8,128)(2,1)}, u32[]{:S(2)}) copy-start(bf16[3072,512]{1,0:T(8,128)(2,1)} %refs_2_.5) | copy-start | bytes 9437188
  22.2 22.3 %copy-start.3 = (f32[128,512]{1,0:T(8,128)S(1)}, f32[128,512]{1,0:T(8,128)}, u32[]{:S(2)}) copy-start(f32[128,512]{1,0:T(8,128)} %get-tuple-element.13.refs_1_) | copy-start | bytes 786436
  47.5 5.0 %copy-start.5 = (bf16[128,3072]{1,0:T(8,128)(2,1)S(1)}, bf16[128,3072]{1,0:T(8,128)(2,1)}, u32[]{:S(2)}) copy-start(bf16[128,3072]{1,0:T(8,128)(2,1)} %refs_4_.1) | copy-start | bytes 2359300
  47.5 15.9 %all-to-all-start.2 = ((bf16[16,200,128]{2,1,0:T(8,128)(2,1)}), bf16[16,200,128]{2,1,0:T(8,128)(2,1)S(1)}, u32[]{:S(2)}, u32[]{:S(2)}) async-start(bf16[16,200,128]{2,1,0:T(8,128)(2,1)} %get-tuple-element.14), calls=%async_computation.2 | async-start | bytes 1638400 | tf_op jit(solution)/shard_map/all_to_all | solution.py:363
  52.6 1.8 %collective-permute-start = (bf16[128,1536]{1,0:T(8,128)(2,1)S(1)}, bf16[128,1536]{1,0:T(8,128)(2,1)S(1)}, u32[]{:S(2)}, u32[]{:S(2)}) collective-permute-start(bf16[128,1536]{1,0:T(8,128)(2,1)S(1)} %get-tuple-element.21), channel_id=1, source_target_pairs={{0,128},{128,0},{1,129},{129,1},{2,130},{130,2},{3,131},{131,3},{4... | collective-permute-start | bytes 1179656 | tf_op jit(solution)/shard_map/ppermute | solution.py:280
  52.7 1.9 %collective-permute-start.1 = (bf16[128,512]{1,0:T(8,128)(2,1)S(1)}, bf16[128,512]{1,0:T(8,128)(2,1)S(1)}, u32[]{:S(2)}, u32[]{:S(2)}) collective-permute-start(bf16[128,512]{1,0:T(8,128)(2,1)S(1)} %get-tuple-element.15.grad_mine), channel_id=1, source_target_pairs={{0,128},{128,0},{1,129},{129,1},{2,130},{130,2},{3,131},{131,3},{4... | collective-permute-start | bytes 393224 | tf_op jit(solution)/shard_map/ppermute | solution.py:362

commit v5 on v4

--- a/solution.py
+++ b/solution.py
@@ -13,6 +13,8 @@
 F32 = jnp.float32
 BF16 = jnp.bfloat16
 EXTRA = 8
+FIRST_OWNER = 10
+FIRST_SVOC = 4
 
 
 def vmem():
@@ -29,6 +31,10 @@
 
 def as_row(tile):
     return jnp.sum(tile.T, axis=0, keepdims=True)
+
+
+def turned(length, first):
+    return [(k + first) % length for k in range(length)]
 
 
 def lane_blocks(array, width=128):
@@ -152,13 +158,13 @@
         at = pl.multiple_of(row * blk, blk)
         block = jnp.dot(probs[:, pl.ds(at, blk)], values[s], preferred_element_type=F32)
         mapped[place[s]] += block
-    for o in range(owners):
+    for k, o in enumerate(turned(owners, FIRST_OWNER)):
         for c in range(CAP):
-            outgoing[o, c * blk : (c + 1) * blk, :] = mapped[o * CAP + c].astype(BF16)
+            outgoing[k, c * blk : (c + 1) * blk, :] = mapped[o * CAP + c].astype(BF16)
         label_a = lax.rem(jnp.maximum(first[o], 0), per_owner).astype(F32)
         label_b = lax.rem(jnp.maximum(second[o], 0), per_owner).astype(F32)
         at = lax.broadcasted_iota(jnp.int32, (EXTRA, blk), 0)
-        outgoing[o, CAP * blk :, :] = jnp.where(
+        outgoing[k, CAP * blk :, :] = jnp.where(
             at == 0, label_a, jnp.where(at == 1, label_b, 0.0)
         ).astype(BF16)
 
@@ -219,6 +225,7 @@
     tail = rows_of(sums, EXTRA, blk).astype(BF16)
     owners, height = outgoing.shape[0], outgoing.shape[1] - EXTRA
     step = owners // chunks
+    place = turned(owners, owners - FIRST_OWNER)
     grads = grad[...]
     for k in range(chunks):
         rows = lax.dot_general(
@@ -226,8 +233,9 @@
             (((1,), (1,)), ((), ())), preferred_element_type=F32,
         ).astype(BF16)
         for o in range(step):
-            outgoing[k * step + o, :height, :] = rows[o * height : (o + 1) * height]
-            outgoing[k * step + o, height:, :] = tail
+            at = place[k * step + o]
+            outgoing[at, :height, :] = rows[o * height : (o + 1) * height]
+            outgoing[at, height:, :] = tail
 
 
 def head_kernel(mine, other, grad_mine, grad_other, out):
@@ -249,9 +257,9 @@
         for part in in_parts(jnp.sum(total[at : at + 3], axis=0, keepdims=True))
     ]
     tail = rows_of(sums, EXTRA, total.shape[1]).astype(BF16)
-    for o in range(owners):
-        outgoing[o, :height, :] = total[o * height : (o + 1) * height].astype(BF16)
-        outgoing[o, height:, :] = tail
+    for k, o in enumerate(turned(owners, FIRST_SVOC)):
+        outgoing[k, :height, :] = total[o * height : (o + 1) * height].astype(BF16)
+        outgoing[k, height:, :] = tail
 
 
 def last_sum_kernel(received, finals, divergence, grad_hidden):
@@ -276,6 +284,8 @@
     half = width // lax.axis_size("dp")
     me = lax.axis_index("dp")
     swap = [(0, 1), (1, 0)]
+    tvoc_order = [turned(owners, FIRST_OWNER)]
+    svoc_order = [turned(svocs, FIRST_SVOC)]
     hidden_mine = lax.dynamic_slice_in_dim(hidden, me * half, half, 1)
     hidden_other = lax.ppermute(
         lax.dynamic_slice_in_dim(hidden, (1 - me) * half, half, 1), "dp", swap
@@ -304,7 +314,7 @@
         compiler_params=params(60),
         name="stats",
     )(index, block_count, teacher_probs, values, hidden, student_weight)
-    near_stats = lax.all_to_all(stats, "svoc", 0, 0, tiled=True)
+    near_stats = lax.all_to_all(stats, "svoc", 0, 0, tiled=True, axis_index_groups=svoc_order)
 
     def mapping(*refs):
         mapping_kernel(slots, owners, per_owner, *refs)
@@ -341,7 +351,7 @@
         compiler_params=params(),
         name="tail",
     )(near_stats, outgoing)
-    received = lax.all_to_all(outgoing, TVOC, 0, 0, tiled=True)
+    received = lax.all_to_all(outgoing, TVOC, 0, 0, tiled=True, axis_index_groups=tvoc_order)
     height = width // owners
 
     def middle(*refs):
@@ -360,7 +370,9 @@
         name="middle",
     )(received, logits, student_weight)
     grad_other = lax.ppermute(grad, "dp", swap)
-    summed = lax.all_to_all(partial_hidden, TVOC, 0, 0, tiled=True)
+    summed = lax.all_to_all(
+        partial_hidden, TVOC, 0, 0, tiled=True, axis_index_groups=tvoc_order
+    )
     tiles = 4
     grad_weight = pl.pallas_call(
         head_kernel,
@@ -386,7 +398,7 @@
         compiler_params=params(),
         name="half_sum",
     )(summed)
-    arrived = lax.all_to_all(nearer, "svoc", 0, 0, tiled=True)
+    arrived = lax.all_to_all(nearer, "svoc", 0, 0, tiled=True, axis_index_groups=svoc_order)
     divergence, grad_hidden = pl.pallas_call(
         last_sum_kernel,
         out_shape=(shape((1, tokens), F32), shape((last, tokens), F32)),

time: 75.2 us -> 70.7 us (0.940)
  waiting for transfers between devices: 13.7 us -> 6.67 us
  starting transfers between devices: 14.1 us -> 18.4 us
  blocking collectives: 33.1 us -> 30.8 us
    all_to_all x2, waiting for transfers between devices: 12.3 us -> 5.27 us  [the longest x1 4.36 us: local(): lax.all_to_all(partial_hidden, TVOC, 0, 0, tiled=True, axis_index_groups=...]
    all_to_all x2, starting transfers between devices: 13.5 us -> 17.8 us  [the longest x1 10.5 us: local(): lax.all_to_all(stats, 'svoc', 0, 0, tiled=True, axis_index_groups=svoc_or...]
    all_to_all x2, blocking collectives: 33.1 us -> 30.8 us  [the longest x1 20.4 us: local(): lax.all_to_all(outgoing, TVOC, 0, 0, tiled=True, axis_index_groups=tvoc_o...]
where the time goes in v5:
time: 70.7 us; the launch traced here: 69.9 us
  blocking collectives  30.8 us (44%)
  starting transfers between devices  18.4 us (26%)
  Pallas kernels  12.6 us (18%)
  waiting for transfers between devices  6.67 us (9%)
  between operations  1.37 us (2%)
    all_to_all x1, blocking collectives, local(): lax.all_to_all(outgoing, TVOC, 0, 0, tiled=True, axis_index_groups=tvoc_o...  20.4 us
    all_to_all x1, starting transfers between devices, local(): lax.all_to_all(stats, 'svoc', 0, 0, tiled=True, axis_index_groups=svoc_or...  10.5 us
    all_to_all x1, blocking collectives, local(): lax.all_to_all(nearer, 'svoc', 0, 0, tiled=True, axis_index_groups=svoc_o...  10.4 us
    all_to_all x1, starting transfers between devices, local(): lax.all_to_all(partial_hidden, TVOC, 0, 0, tiled=True, axis_index_groups=...  7.33 us
    pallas_call x1, Pallas kernels, local(): pl.pallas_call(stats_of, out_shape=(shape((tokens, shard), F32), shape((s...  4.59 us
    all_to_all x1, waiting for transfers between devices, local(): lax.all_to_all(partial_hidden, TVOC, 0, 0, tiled=True, axis_index_groups=...  4.36 us
    pallas_call x1, Pallas kernels, local(): pl.pallas_call(middle, out_shape=(shape((tokens, shard), BF16), shape((ow...  2.95 us
    pallas_call x1, Pallas kernels, local(): pl.pallas_call(head_kernel, out_shape=shape((half, shard), BF16), grid=(t...  2.77 us
  transfers between devices with their start and end apart: 4, of which 4 were waited for; matrix products, arithmetic and copies ran while one was open for 0% of the time, Pallas kernels for 6%

profile of v5, /device:TPU:8, one launch (start us, length us, event | category | flops | bytes accessed | tf_op | source)
XLA Modules:
  0.0 69.9 jit_solution(5072734120636231482)
XLA Ops:
  1.3 0.0 copy-start.1
  1.3 0.0 copy-start.2
  1.3 0.0 copy-start.4
  1.3 4.6 %stats.1 = (f32[128,512]{1,0:T(8,128)}, f32[8,2,128]{2,1,0:T(2,128)}) custom-call(s32[2,24]{1,0:T(2,128)} %bitcast.8, s32[1,1]{1,0:T(1,128)S(6)} %copy.11.refs_1_, bf16[128,5120]{1,0:T(8,128)(2,1)} %refs_2_.4, bf16[24,128,128]{2,1,0:T(8,128)(2,1)} %bitcast.6, bf16[128,3072]{1,0:T(8,128)(2,1)} %refs_4_.1, bf16[3072,512]{1,0:T(8,128)(2,1)} %refs_2_.5), custom_call_target="tpu_custom_call" | custom-call | tf_op jit(solution)/shard_map/stats/pallas_call | solution.py:299
  5.9 10.5 %all-to-all-start = ((f32[8,2,128]{2,1,0:T(2,128)}), f32[8,2,128]{2,1,0:T(2,128)S(1)}, u32[]{:S(2)}, u32[]{:S(2)}) async-start(f32[8,2,128]{2,1,0:T(2,128)} %get-tuple-element.12), calls=%async_computation | async-start | bytes 16384 | tf_op jit(solution)/shard_map/all_to_all | solution.py:317
  16.4 0.0 copy-done.1
  16.4 0.0 copy-done.2
  16.4 1.4 %mapping.1._ = bf16[16,264,128]{2,1,0:T(8,128)(2,1)S(1)} custom-call(s32[2,24]{1,0:T(2,128)S(1)} %bitcast.9, s32[1,1]{1,0:T(1,128)S(6)} %copy.11.refs_1_, bf16[128,5120]{1,0:T(8,128)(2,1)S(1)} %copy-done.1, bf16[24,128,128]{2,1,0:T(8,128)(2,1)S(1)} %bitcast.7), custom_call_target="tpu_custom_call" | custom-call | flops 100663296 | bytes 4194304 | tf_op jit(solution)/shard_map/mapping/pallas_call | solution.py:322
  17.8 0.9 %all-to-all-done.stats = f32[8,2,128]{2,1,0:T(2,128)S(1)} async-done(((f32[8,2,128]{2,1,0:T(2,128)}), f32[8,2,128]{2,1,0:T(2,128)S(1)}, u32[]{:S(2)}, u32[]{:S(2)}) %all-to-all-start) | async-done | bytes 8224 | tf_op jit(solution)/shard_map/all_to_all | solution.py:317
  18.8 0.1 tail.1
  18.9 0.0 copy-start.3
  18.9 20.4 %all_to_all.20.refs_0_ = bf16[16,264,128]{2,1,0:T(8,128)(2,1)S(1)} all-to-all(bf16[16,264,128]{2,1,0:T(8,128)(2,1)S(1)} %tail.1), channel_id=1, replica_groups={{80,88,96,104,112,120,0,8,16,24,32,40,48,56,64,72},{81,89,97,105,113,12..., dimensions={0} | all-to-all | bytes 2162688 | tf_op jit(solution)/shard_map/all_to_all | solution.py:354
  39.3 3.0 %middle.1 = (bf16[128,512]{1,0:T(8,128)(2,1)S(1)}, bf16[16,200,128]{2,1,0:T(8,128)(2,1)}, f32[1,128]{1,0:T(1,128)S(1)}) custom-call(bf16[16,264,128]{2,1,0:T(8,128)(2,1)S(1)} %all_to_all.20.refs_0_, f32[128,512]{1,0:T(8,128)S(1)} %copy-done.3, bf16[3072,512]{1,0:T(8,128)(2,1)S(1)} %copy-done), custom_call_target="tpu_custom_call" | custom-call | tf_op jit(solution)/shard_map/middle/pallas_call | solution.py:360
  42.2 7.3 %all-to-all-start.2 = ((bf16[16,200,128]{2,1,0:T(8,128)(2,1)}), bf16[16,200,128]{2,1,0:T(8,128)(2,1)S(1)}, u32[]{:S(2)}, u32[]{:S(2)}) async-start(bf16[16,200,128]{2,1,0:T(8,128)(2,1)} %get-tuple-element.14), calls=%async_computation.2 | async-start | bytes 1638400 | tf_op jit(solution)/shard_map/all_to_all | solution.py:373
  49.6 0.1 constant_dynamic-slice_fusion
  49.6 0.1 collective-permute-start
  49.7 0.5 collective-permute-start.1
  50.2 1.2 %collective-permute-done.other = bf16[128,1536]{1,0:T(8,128)(2,1)S(1)} collective-permute-done((bf16[128,1536]{1,0:T(8,128)(2,1)S(1)}, bf16[128,1536]{1,0:T(8,128)(2,1)S(1)}, u32[]{:S(2)}, u32[]{:S(2)}) %collective-permute-start) | collective-permute-done | bytes 393248 | tf_op jit(solution)/shard_map/ppermute | solution.py:290
  51.5 0.2 collective-permute-done.1.grad_other
  51.6 2.8 %head.1 = bf16[1536,512]{1,0:T(8,128)(2,1)} custom-call(bf16[128,1536]{1,0:T(8,128)(2,1)S(1)} %get-tuple-element.22.mine, bf16[128,1536]{1,0:T(8,128)(2,1)S(1)} %collective-permute-done.other, bf16[128,512]{1,0:T(8,128)(2,1)S(1)} %get-tuple-element.15.grad_mine, bf16[128,512]{1,0:T(8,128)(2,1)S(1)} %collective-permute-done.1.grad_other), custom_call_target="tpu_custom_call" | custom-call | tf_op jit(solution)/shard_map/head/pallas_call | solution.py:377
  54.4 4.4 %all-to-all-done.2.received = bf16[16,200,128]{2,1,0:T(8,128)(2,1)S(1)} async-done(((bf16[16,200,128]{2,1,0:T(8,128)(2,1)}), bf16[16,200,128]{2,1,0:T(8,128)(2,1)S(1)}, u32[]{:S(2)}, u32[]{:S(2)}) %all-to-all-start.2) | async-done | bytes 819232 | tf_op jit(solution)/shard_map/all_to_all | solution.py:373
  58.8 0.1 half_sum.1
  58.9 10.4 %all_to_all.21.received = bf16[8,32,128]{2,1,0:T(8,128)(2,1)S(1)} all-to-all(bf16[8,32,128]{2,1,0:T(8,128)(2,1)S(1)} %half_sum.1), channel_id=1, replica_groups={{4,5,6,7,0,1,2,3},{12,13,14,15,8,9,10,11},{20,21,22,23,16,17,18,19},{28..., dimensions={0} | all-to-all | bytes 131072 | tf_op jit(solution)/shard_map/all_to_all | solution.py:401
  69.3 0.6 last_sum.1
  (6 shorter events, 0.0 us)
Async XLA Ops:
  1.3 15.1 %copy-start.1 = (bf16[128,5120]{1,0:T(8,128)(2,1)S(1)}, bf16[128,5120]{1,0:T(8,128)(2,1)}, u32[]{:S(2)}) copy-start(bf16[128,5120]{1,0:T(8,128)(2,1)} %refs_2_.4) | copy-start | bytes 3932164
  1.3 15.1 %copy-start.2 = (bf16[1,1,24,128,128]{4,3,2,1,0:T(8,128)(2,1)S(1)}, bf16[1,1,24,128,128]{4,3,2,1,0:T(8,128)(2,1)}, u32[]{:S(2)}) copy-start(bf16[1,1,24,128,128]{4,3,2,1,0:T(8,128)(2,1)} %param.7) | copy-start | bytes 2359300
  1.3 15.1 %copy-start.4 = (s32[1,1,24,2]{2,3,1,0:T(2,128)S(1)}, s32[1,1,24,2]{2,3,1,0:T(2,128)}, u32[]{:S(2)}) copy-start(s32[1,1,24,2]{2,3,1,0:T(2,128)} %param.8) | copy-start | bytes 580
  5.9 12.9 %all-to-all-start = ((f32[8,2,128]{2,1,0:T(2,128)}), f32[8,2,128]{2,1,0:T(2,128)S(1)}, u32[]{:S(2)}, u32[]{:S(2)}) async-start(f32[8,2,128]{2,1,0:T(2,128)} %get-tuple-element.12), calls=%async_computation | async-start | bytes 16384 | tf_op jit(solution)/shard_map/all_to_all | solution.py:317
  18.8 20.5 %copy-start = (bf16[3072,512]{1,0:T(8,128)(2,1)S(1)}, bf16[3072,512]{1,0:T(8,128)(2,1)}, u32[]{:S(2)}) copy-start(bf16[3072,512]{1,0:T(8,128)(2,1)} %refs_2_.5) | copy-start | bytes 9437188
  18.9 20.4 %copy-start.3 = (f32[128,512]{1,0:T(8,128)S(1)}, f32[128,512]{1,0:T(8,128)}, u32[]{:S(2)}) copy-start(f32[128,512]{1,0:T(8,128)} %get-tuple-element.13.refs_1_) | copy-start | bytes 786436
  42.2 7.3 %copy-start.5 = (bf16[128,3072]{1,0:T(8,128)(2,1)S(1)}, bf16[128,3072]{1,0:T(8,128)(2,1)}, u32[]{:S(2)}) copy-start(bf16[128,3072]{1,0:T(8,128)(2,1)} %refs_4_.1) | copy-start | bytes 2359300
  42.2 16.5 %all-to-all-start.2 = ((bf16[16,200,128]{2,1,0:T(8,128)(2,1)}), bf16[16,200,128]{2,1,0:T(8,128)(2,1)S(1)}, u32[]{:S(2)}, u32[]{:S(2)}) async-start(bf16[16,200,128]{2,1,0:T(8,128)(2,1)} %get-tuple-element.14), calls=%async_computation.2 | async-start | bytes 1638400 | tf_op jit(solution)/shard_map/all_to_all | solution.py:373
  49.6 1.8 %collective-permute-start = (bf16[128,1536]{1,0:T(8,128)(2,1)S(1)}, bf16[128,1536]{1,0:T(8,128)(2,1)S(1)}, u32[]{:S(2)}, u32[]{:S(2)}) collective-permute-start(bf16[128,1536]{1,0:T(8,128)(2,1)S(1)} %get-tuple-element.21), channel_id=1, source_target_pairs={{0,128},{128,0},{1,129},{129,1},{2,130},{130,2},{3,131},{131,3},{4... | collective-permute-start | bytes 1179656 | tf_op jit(solution)/shard_map/ppermute | solution.py:290
  49.7 1.9 %collective-permute-start.1 = (bf16[128,512]{1,0:T(8,128)(2,1)S(1)}, bf16[128,512]{1,0:T(8,128)(2,1)S(1)}, u32[]{:S(2)}, u32[]{:S(2)}) collective-permute-start(bf16[128,512]{1,0:T(8,128)(2,1)S(1)} %get-tuple-element.15.grad_mine), channel_id=1, source_target_pairs={{0,128},{128,0},{1,129},{129,1},{2,130},{130,2},{3,131},{131,3},{4... | collective-permute-start | bytes 393224 | tf_op jit(solution)/shard_map/ppermute | solution.py:372

commit v6 on v5

--- a/solution.py
+++ b/solution.py
@@ -14,7 +14,7 @@
 BF16 = jnp.bfloat16
 EXTRA = 8
 FIRST_OWNER = 10
-FIRST_SVOC = 4
+SVOC_ORDER = [4, 0, 7, 1, 6, 2, 5, 3]
 
 
 def vmem():
@@ -257,7 +257,7 @@
         for part in in_parts(jnp.sum(total[at : at + 3], axis=0, keepdims=True))
     ]
     tail = rows_of(sums, EXTRA, total.shape[1]).astype(BF16)
-    for k, o in enumerate(turned(owners, FIRST_SVOC)):
+    for k, o in enumerate(SVOC_ORDER):
         outgoing[k, :height, :] = total[o * height : (o + 1) * height].astype(BF16)
         outgoing[k, height:, :] = tail
 
@@ -277,6 +277,7 @@
     tokens, width = hidden.shape
     slots, blk = block_values.shape[2], block_values.shape[-1]
     owners, svocs = lax.axis_size(TVOC), lax.axis_size("svoc")
+    assert svocs == len(SVOC_ORDER)
     shard = student_weight.shape[1]
     per_owner = shard // blk
     shape = jax.ShapeDtypeStruct
@@ -285,7 +286,7 @@
     me = lax.axis_index("dp")
     swap = [(0, 1), (1, 0)]
     tvoc_order = [turned(owners, FIRST_OWNER)]
-    svoc_order = [turned(svocs, FIRST_SVOC)]
+    svoc_order = [SVOC_ORDER]
     hidden_mine = lax.dynamic_slice_in_dim(hidden, me * half, half, 1)
     hidden_other = lax.ppermute(
         lax.dynamic_slice_in_dim(hidden, (1 - me) * half, half, 1), "dp", swap
@@ -373,7 +374,7 @@
     summed = lax.all_to_all(
         partial_hidden, TVOC, 0, 0, tiled=True, axis_index_groups=tvoc_order
     )
-    tiles = 4
+    tiles = 2
     grad_weight = pl.pallas_call(
         head_kernel,
         out_shape=shape((half, shard), BF16),

time: 70.7 us -> 70.6 us (level)
  transfers between devices with their start and end apart: 4 -> 4, of which waited for: 4 -> 4; matrix products, arithmetic and copies ran while one was open for 0% -> 0% of each run, Pallas kernels for 6% -> 5%
where the time goes in v6:
time: 70.6 us; the launch traced here: 69.8 us
  blocking collectives  30.7 us (43%)
  starting transfers between devices  18.4 us (26%)
  Pallas kernels  12 us (17%)
  waiting for transfers between devices  7.29 us (10%)
  between operations  1.37 us (2%)
    all_to_all x1, blocking collectives, local(): lax.all_to_all(outgoing, TVOC, 0, 0, tiled=True, axis_index_groups=tvoc_o...  20.4 us
    all_to_all x1, starting transfers between devices, local(): lax.all_to_all(stats, 'svoc', 0, 0, tiled=True, axis_index_groups=svoc_or...  10.4 us
    all_to_all x1, blocking collectives, local(): lax.all_to_all(nearer, 'svoc', 0, 0, tiled=True, axis_index_groups=svoc_o...  10.3 us
    all_to_all x1, starting transfers between devices, local(): lax.all_to_all(partial_hidden, TVOC, 0, 0, tiled=True, axis_index_groups=...  7.33 us
    all_to_all x1, waiting for transfers between devices, local(): lax.all_to_all(partial_hidden, TVOC, 0, 0, tiled=True, axis_index_groups=...  4.97 us
    pallas_call x1, Pallas kernels, local(): pl.pallas_call(stats_of, out_shape=(shape((tokens, shard), F32), shape((s...  4.59 us
    pallas_call x1, Pallas kernels, local(): pl.pallas_call(middle, out_shape=(shape((tokens, shard), BF16), shape((ow...  2.95 us
    pallas_call x1, Pallas kernels, local(): pl.pallas_call(head_kernel, out_shape=shape((half, shard), BF16), grid=(t...  2.17 us
  transfers between devices with their start and end apart: 4, of which 4 were waited for; matrix products, arithmetic and copies ran while one was open for 0% of the time, Pallas kernels for 5%

profile of v6, /device:TPU:8, one launch (start us, length us, event | category | flops | bytes accessed | tf_op | source)
XLA Modules:
  0.0 69.8 jit_solution(9616265837431599547)
XLA Ops:
  1.3 0.0 copy-start.1
  1.3 4.6 %stats.1 = (f32[128,512]{1,0:T(8,128)}, f32[8,2,128]{2,1,0:T(2,128)}) custom-call(s32[2,24]{1,0:T(2,128)} %bitcast.8, s32[1,1]{1,0:T(1,128)S(6)} %copy.11.refs_1_, bf16[128,5120]{1,0:T(8,128)(2,1)} %refs_2_.4, bf16[24,128,128]{2,1,0:T(8,128)(2,1)} %bitcast.6, bf16[128,3072]{1,0:T(8,128)(2,1)} %refs_4_.1, bf16[3072,512]{1,0:T(8,128)(2,1)} %refs_2_.5), custom_call_target="tpu_custom_call" | custom-call | tf_op jit(solution)/shard_map/stats/pallas_call | solution.py:300
  5.9 10.4 %all-to-all-start = ((f32[8,2,128]{2,1,0:T(2,128)}), f32[8,2,128]{2,1,0:T(2,128)S(1)}, u32[]{:S(2)}, u32[]{:S(2)}) async-start(f32[8,2,128]{2,1,0:T(2,128)} %get-tuple-element.12), calls=%async_computation | async-start | bytes 16384 | tf_op jit(solution)/shard_map/all_to_all | solution.py:318
  16.3 0.0 copy-done.2
  16.4 0.0 copy-done.4
  16.4 1.5 %mapping.1._ = bf16[16,264,128]{2,1,0:T(8,128)(2,1)S(1)} custom-call(s32[2,24]{1,0:T(2,128)S(1)} %bitcast.9, s32[1,1]{1,0:T(1,128)S(6)} %copy.11.refs_1_, bf16[128,5120]{1,0:T(8,128)(2,1)S(1)} %copy-done.1, bf16[24,128,128]{2,1,0:T(8,128)(2,1)S(1)} %bitcast.7), custom_call_target="tpu_custom_call" | custom-call | flops 100663296 | bytes 4194304 | tf_op jit(solution)/shard_map/mapping/pallas_call | solution.py:323
  17.8 0.9 %all-to-all-done.stats = f32[8,2,128]{2,1,0:T(2,128)S(1)} async-done(((f32[8,2,128]{2,1,0:T(2,128)}), f32[8,2,128]{2,1,0:T(2,128)S(1)}, u32[]{:S(2)}, u32[]{:S(2)}) %all-to-all-start) | async-done | bytes 8224 | tf_op jit(solution)/shard_map/all_to_all | solution.py:318
  18.7 0.1 tail.1
  18.8 0.0 copy-start.3
  18.9 20.4 %all_to_all.20.refs_0_ = bf16[16,264,128]{2,1,0:T(8,128)(2,1)S(1)} all-to-all(bf16[16,264,128]{2,1,0:T(8,128)(2,1)S(1)} %tail.1), channel_id=1, replica_groups={{80,88,96,104,112,120,0,8,16,24,32,40,48,56,64,72},{81,89,97,105,113,12..., dimensions={0} | all-to-all | bytes 2162688 | tf_op jit(solution)/shard_map/all_to_all | solution.py:355
  39.3 0.0 copy-done
  39.3 3.0 %middle.1 = (bf16[128,512]{1,0:T(8,128)(2,1)S(1)}, bf16[16,200,128]{2,1,0:T(8,128)(2,1)}, f32[1,128]{1,0:T(1,128)S(1)}) custom-call(bf16[16,264,128]{2,1,0:T(8,128)(2,1)S(1)} %all_to_all.20.refs_0_, f32[128,512]{1,0:T(8,128)S(1)} %copy-done.3, bf16[3072,512]{1,0:T(8,128)(2,1)S(1)} %copy-done), custom_call_target="tpu_custom_call" | custom-call | tf_op jit(solution)/shard_map/middle/pallas_call | solution.py:361
  42.2 7.3 %all-to-all-start.2 = ((bf16[16,200,128]{2,1,0:T(8,128)(2,1)}), bf16[16,200,128]{2,1,0:T(8,128)(2,1)S(1)}, u32[]{:S(2)}, u32[]{:S(2)}) async-start(bf16[16,200,128]{2,1,0:T(8,128)(2,1)} %get-tuple-element.14), calls=%async_computation.2 | async-start | bytes 1638400 | tf_op jit(solution)/shard_map/all_to_all | solution.py:374
  49.6 0.0 copy-done.5
  49.6 0.1 constant_dynamic-slice_fusion
  49.6 0.1 collective-permute-start
  49.7 0.5 collective-permute-start.1
  50.2 1.2 %collective-permute-done.other = bf16[128,1536]{1,0:T(8,128)(2,1)S(1)} collective-permute-done((bf16[128,1536]{1,0:T(8,128)(2,1)S(1)}, bf16[128,1536]{1,0:T(8,128)(2,1)S(1)}, u32[]{:S(2)}, u32[]{:S(2)}) %collective-permute-start) | collective-permute-done | bytes 393248 | tf_op jit(solution)/shard_map/ppermute | solution.py:291
  51.5 0.2 collective-permute-done.1.grad_other
  51.6 2.2 %head.1 = bf16[1536,512]{1,0:T(8,128)(2,1)} custom-call(bf16[128,1536]{1,0:T(8,128)(2,1)S(1)} %get-tuple-element.22.mine, bf16[128,1536]{1,0:T(8,128)(2,1)S(1)} %collective-permute-done.other, bf16[128,512]{1,0:T(8,128)(2,1)S(1)} %get-tuple-element.15.grad_mine, bf16[128,512]{1,0:T(8,128)(2,1)S(1)} %collective-permute-done.1.grad_other), custom_call_target="tpu_custom_call" | custom-call | tf_op jit(solution)/shard_map/head/pallas_call | solution.py:378
  53.8 5.0 %all-to-all-done.2.received = bf16[16,200,128]{2,1,0:T(8,128)(2,1)S(1)} async-done(((bf16[16,200,128]{2,1,0:T(8,128)(2,1)}), bf16[16,200,128]{2,1,0:T(8,128)(2,1)S(1)}, u32[]{:S(2)}, u32[]{:S(2)}) %all-to-all-start.2) | async-done | bytes 819232 | tf_op jit(solution)/shard_map/all_to_all | solution.py:374
  58.8 0.1 half_sum.1
  58.9 10.3 %all_to_all.21.received = bf16[8,32,128]{2,1,0:T(8,128)(2,1)S(1)} all-to-all(bf16[8,32,128]{2,1,0:T(8,128)(2,1)S(1)} %half_sum.1), channel_id=1, replica_groups={{4,0,7,1,6,2,5,3},{12,8,15,9,14,10,13,11},{20,16,23,17,22,18,21,19},{28..., dimensions={0} | all-to-all | bytes 131072 | tf_op jit(solution)/shard_map/all_to_all | solution.py:402
  69.2 0.6 last_sum.1
  (6 shorter events, 0.0 us)
Async XLA Ops:
  1.3 15.1 %copy-start.1 = (bf16[128,5120]{1,0:T(8,128)(2,1)S(1)}, bf16[128,5120]{1,0:T(8,128)(2,1)}, u32[]{:S(2)}) copy-start(bf16[128,5120]{1,0:T(8,128)(2,1)} %refs_2_.4) | copy-start | bytes 3932164
  1.3 15.1 %copy-start.2 = (bf16[1,1,24,128,128]{4,3,2,1,0:T(8,128)(2,1)S(1)}, bf16[1,1,24,128,128]{4,3,2,1,0:T(8,128)(2,1)}, u32[]{:S(2)}) copy-start(bf16[1,1,24,128,128]{4,3,2,1,0:T(8,128)(2,1)} %param.7) | copy-start | bytes 2359300
  1.3 15.1 %copy-start.4 = (s32[1,1,24,2]{2,3,1,0:T(2,128)S(1)}, s32[1,1,24,2]{2,3,1,0:T(2,128)}, u32[]{:S(2)}) copy-start(s32[1,1,24,2]{2,3,1,0:T(2,128)} %param.8) | copy-start | bytes 580
  5.9 12.8 %all-to-all-start = ((f32[8,2,128]{2,1,0:T(2,128)}), f32[8,2,128]{2,1,0:T(2,128)S(1)}, u32[]{:S(2)}, u32[]{:S(2)}) async-start(f32[8,2,128]{2,1,0:T(2,128)} %get-tuple-element.12), calls=%async_computation | async-start | bytes 16384 | tf_op jit(solution)/shard_map/all_to_all | solution.py:318
  18.7 20.5 %copy-start = (bf16[3072,512]{1,0:T(8,128)(2,1)S(1)}, bf16[3072,512]{1,0:T(8,128)(2,1)}, u32[]{:S(2)}) copy-start(bf16[3072,512]{1,0:T(8,128)(2,1)} %refs_2_.5) | copy-start | bytes 9437188
  18.8 20.4 %copy-start.3 = (f32[128,512]{1,0:T(8,128)S(1)}, f32[128,512]{1,0:T(8,128)}, u32[]{:S(2)}) copy-start(f32[128,512]{1,0:T(8,128)} %get-tuple-element.13.refs_1_) | copy-start | bytes 786436
  42.2 7.3 %copy-start.5 = (bf16[128,3072]{1,0:T(8,128)(2,1)S(1)}, bf16[128,3072]{1,0:T(8,128)(2,1)}, u32[]{:S(2)}) copy-start(bf16[128,3072]{1,0:T(8,128)(2,1)} %refs_4_.1) | copy-start | bytes 2359300
  42.2 16.5 %all-to-all-start.2 = ((bf16[16,200,128]{2,1,0:T(8,128)(2,1)}), bf16[16,200,128]{2,1,0:T(8,128)(2,1)S(1)}, u32[]{:S(2)}, u32[]{:S(2)}) async-start(bf16[16,200,128]{2,1,0:T(8,128)(2,1)} %get-tuple-element.14), calls=%async_computation.2 | async-start | bytes 1638400 | tf_op jit(solution)/shard_map/all_to_all | solution.py:374
  49.6 1.8 %collective-permute-start = (bf16[128,1536]{1,0:T(8,128)(2,1)S(1)}, bf16[128,1536]{1,0:T(8,128)(2,1)S(1)}, u32[]{:S(2)}, u32[]{:S(2)}) collective-permute-start(bf16[128,1536]{1,0:T(8,128)(2,1)S(1)} %get-tuple-element.21), channel_id=1, source_target_pairs={{0,128},{128,0},{1,129},{129,1},{2,130},{130,2},{3,131},{131,3},{4... | collective-permute-start | bytes 1179656 | tf_op jit(solution)/shard_map/ppermute | solution.py:291
  49.7 1.9 %collective-permute-start.1 = (bf16[128,512]{1,0:T(8,128)(2,1)S(1)}, bf16[128,512]{1,0:T(8,128)(2,1)S(1)}, u32[]{:S(2)}, u32[]{:S(2)}) collective-permute-start(bf16[128,512]{1,0:T(8,128)(2,1)S(1)} %get-tuple-element.15.grad_mine), channel_id=1, source_target_pairs={{0,128},{128,0},{1,129},{129,1},{2,130},{130,2},{3,131},{131,3},{4... | collective-permute-start | bytes 393224 | tf_op jit(solution)/shard_map/ppermute | solution.py:373
